TPU v7x, 512 devices: a whole 4x8x8 slice. The times are simulated.
512 devices in a mesh: energy: 32 (over y, x), chain: 16 (over z, core).
Axes of the slice: x: 4, y: 8, z: 8, core: 2. Of those that a mesh axis runs over, the one named last changes fastest.
Arguments:
- onsite: float32 [16, 2, 128, 128], P('chain'), may hold values from -0.5 to 0.5
- coupling: float32 [16, 2, 128, 128], P('chain'), may hold values from -0.3125 to 0.3125
- retained: int32 [16, 8192], P('chain'), may hold values from 0 to 16383
Outputs:
- polarization: float32 [2, 32, 16, 8192], P(None, None, 'chain', 'energy')
All inputs are finite; a program needn't handle non-finite values.
Results may differ from a plain program's by a relative error of at most 0.0003.
Values sent between devices are 32-bit elements; how exact they have to be, the bound alone decides.
No kernel may reach another device: no remote copies, remote signals or barrier semaphores. Data moves between devices by JAX's collectives and lax.ppermute only.
A program may use at most 64 MiB of HBM per device.

v0:
```python
import math

import jax
import jax.numpy as jnp
from jax import lax
from jax.sharding import PartitionSpec as P

E_DEV = 1


broadening = 0.04


def shifted_2(value, axis, by):
    peers = lax.axis_size(axis)
    pairs = [(i, i + by) for i in range(peers) if 0 <= i + by < peers]
    return lax.ppermute(value, axis, pairs)


def product(left_part, right_part):
    return jnp.matmul(left_part, right_part, precision=lax.Precision.HIGHEST)


def represent(real_part, imag_part):
    upper_half = jnp.concatenate([real_part, -imag_part], axis=-1)
    lower_half = jnp.concatenate([imag_part, real_part], axis=-1)
    return jnp.concatenate([upper_half, lower_half], axis=-2)


def hermitian(raw_block):
    real_part = 0.5 * (raw_block[0] + raw_block[0].T)
    imag_part = 0.5 * (raw_block[1] - raw_block[1].T)
    return represent(real_part, imag_part)


def contact_term(coupler):
    orbitals = coupler.shape[0] // 2
    square = product(coupler, coupler.T)
    return represent(0.5 * square[orbitals:, :orbitals], -0.5 * square[:orbitals, :orbitals])


def split_parts(matrix, orbitals):
    return jnp.stack([matrix[:orbitals, :orbitals], matrix[orbitals:, :orbitals]])


def invert(matrix):
    normal = product(matrix.T, matrix)
    factor = jnp.linalg.cholesky(normal)
    first = jax.scipy.linalg.cho_solve((factor, True), matrix.T)
    remainder = jnp.eye(matrix.shape[0], dtype=jnp.float32) - product(matrix, first)
    return first + product(first, remainder)


def dft_tables(length):
    positions = jnp.arange(length, dtype=jnp.int32)
    phases = positions[:, None] * positions[None, :] % length
    angles = phases.astype(jnp.float32) * (2.0 * math.pi / length)
    return (jnp.cos(angles), jnp.sin(angles))


def correlate(left_real, left_imag, right_real, right_imag):
    cosine_table, sine_table = dft_tables(left_real.shape[0])
    turn_real = product(cosine_table, left_real) - product(sine_table, left_imag)
    turn_imag = product(cosine_table, left_imag) + product(sine_table, left_real)
    back_real = product(cosine_table, right_real) + product(sine_table, right_imag)
    back_imag = product(cosine_table, right_imag) - product(sine_table, right_real)
    prod_real = turn_real * back_real - turn_imag * back_imag
    prod_imag = turn_real * back_imag + turn_imag * back_real
    inverse_count = 1.0 / left_real.shape[0]
    out_real = (product(cosine_table, prod_real) - product(sine_table, prod_imag)) * inverse_count
    out_imag = (product(cosine_table, prod_imag) + product(sine_table, prod_real)) * inverse_count
    return (out_real, out_imag)


def spectra(received):
    energy_total = received.shape[0]
    column_count = received.shape[1] * received.shape[3]
    columns = [
        received[:, :, part_index, :].reshape(energy_total, column_count) for part_index in range(4)
    ]
    out_real, out_imag = correlate(columns[0], columns[1], columns[2], columns[3])
    return jnp.stack([out_real, out_imag]).reshape(
        2, energy_total, received.shape[1], received.shape[3]
    )


def shards(onsite, coupling, retained):
    orbitals = onsite.shape[-1]
    wide_width = 2 * orbitals
    blocks = onsite.shape[0]
    energy_count = E_DEV
    chains = lax.axis_size("chain")
    position = lax.axis_index("chain")
    groups = lax.axis_size("energy")
    all_energies = energy_count * groups
    offset = lax.axis_index("energy") * energy_count
    energies = (
        -2.0
        + 4.0
        * (offset + jnp.arange(energy_count, dtype=jnp.int32)).astype(jnp.float32)
        / all_energies
    )
    identity = jnp.eye(orbitals, dtype=jnp.float32)
    diagonal_blocks = jax.vmap(hermitian)(onsite)
    couplers = represent(coupling[:, 0], coupling[:, 1])
    at_end = (position == chains - 1).astype(jnp.float32)
    closing = contact_term(couplers[blocks - 1]) * at_end

    def forward(energy, incoming):
        sigma_block = represent(incoming[0], incoming[1])
        shifted = represent(energy * identity, broadening * identity)
        matrix = shifted - diagonal_blocks[0] - sigma_block
        matrix = matrix - closing
        inverse = invert(matrix)
        inverses = [inverse]
        sigma_block = product(product(couplers[0].T, inverse), couplers[0])
        return (jnp.stack(inverses), split_parts(sigma_block, orbitals))

    def backward(local_stack, incoming):
        following = represent(incoming[0], incoming[1])
        full_list = [None] * blocks
        for block_index in reversed(range(blocks)):
            inverse = local_stack[block_index]
            left_part = product(inverse, couplers[block_index])
            right_part = product(couplers[block_index].T, inverse)
            full_list[block_index] = inverse + product(product(left_part, following), right_part)
            following = full_list[block_index]
        return (jnp.stack(full_list), split_parts(following, orbitals))

    greens = jnp.zeros((energy_count, blocks, wide_width, wide_width), jnp.float32)
    full_blocks = jnp.zeros_like(greens)
    empty_all = jnp.zeros((energy_count, 2, orbitals, orbitals), jnp.float32)

    def forward_section(section_index, carried):
        greens_now, outgoing = carried
        incoming = shifted_2(outgoing, "chain", 1)

        def forward_active(received):
            return jax.vmap(forward)(energies, received)

        def forward_waiting(received):
            return (greens_now, outgoing)

        return lax.cond(position == section_index, forward_active, forward_waiting, incoming)

    greens, unused = lax.fori_loop(0, chains, forward_section, (greens, empty_all))

    def backward_section(section_index, carried):
        fulls_now, outgoing = carried
        incoming = shifted_2(outgoing, "chain", -1)

        def backward_active(received):
            return jax.vmap(backward)(greens, received)

        def backward_waiting(received):
            return (fulls_now, outgoing)

        return lax.cond(
            position == chains - 1 - section_index, backward_active, backward_waiting, incoming
        )

    full_blocks, unused = lax.fori_loop(0, chains, backward_section, (full_blocks, empty_all))
    real_flat = full_blocks[:, :, :orbitals, :orbitals].reshape(
        energy_count, blocks, orbitals * orbitals
    )
    imag_flat = full_blocks[:, :, orbitals:, :orbitals].reshape(
        energy_count, blocks, orbitals * orbitals
    )
    mirror = retained % orbitals * orbitals + retained // orbitals
    direct_index = retained[None]
    mirror_index = mirror[None]
    gathered = jnp.stack(
        [
            jnp.take_along_axis(real_flat, direct_index, axis=2),
            jnp.take_along_axis(imag_flat, direct_index, axis=2),
            jnp.take_along_axis(real_flat, mirror_index, axis=2),
            jnp.take_along_axis(imag_flat, mirror_index, axis=2),
        ],
        axis=2,
    )
    return spectra(lax.all_to_all(gathered, "energy", split_axis=3, concat_axis=0, tiled=True))


def solution(mesh):
    in_specs = (P("chain", None, None, None), P("chain", None, None, None), P("chain", None))
    out_specs = P(None, None, "chain", "energy")
    return jax.shard_map(shards, mesh=mesh, in_specs=in_specs, out_specs=out_specs, check_vma=False)
```

profile of v0, /device:TPU:8, one launch (start us, length us, event | category | flops | bytes accessed | tf_op | source)
XLA Modules:
  0.0 1574.5 jit_solution(14533589909469045075)
XLA Ops:
  6.1 599.1 %while.35 = (s32[]{:T(128)}, f32[1,1,256,256]{3,2,1,0:T(8,128)}, f32[1,2,128,128]{3,2,1,0:T(8,128)S(1)}, s32[]{:T(128)}, f32[1]{0:T(128)}, /*index=5*/f32[1,256,...) while((s32[]{:T(128)}, f32[1,1,256,256]{3,2,1,0:T(8,128)}, ...), condition=%wide.region_7.8_spmd.clone.clone, body=%wide.region_0.7_spmd.clone.clone.sunk | while | flops 1360756992 | bytes 12716502 | solution.py:146
  8.9 66.7 %conditional.7 = ((f32[1,1,256,256]{3,2,1,0:T(8,128)}, f32[1,2,128,128]{3,2,1,0:T(8,128)S(1)})) conditional(s32[]{:T(128)} %convert_element_type.94, (f32[1,1,256,256]{3,2,1,0:T(8,128)}, f32[1,2,128,128]{3,2,1,0:T(8,128)S(1)}) %tuple.114, (f32[1]{0:T(128)}, f32[128,128]{0,1:T(8,128)S(1)}, f32[128,128]{0,1:T(8,128)S(1)}, f32[128,128]{0,1:T(8,128)S(1)}, ...), branch_computations={%region_1.0_spmd, %region_2.6_spmd} | conditional | flops 1360724224 | bytes 11864299 | solution.py:144
  9.7 11.7 custom-call.16
  22.2 9.8 custom-call.17
  32.5 11.7 custom-call.18
  46.2 4.1 while.33
  50.3 19.7 %custom-call.19 = f32[1,2,128,128]{2,3,1,0:T(8,128)S(1)} custom-call(f32[1,2,128,128]{3,2,1,0:T(8,128)S(1)} %bitcast.264), custom_call_target="InvertDiagBlocksLowerTriangular" | custom-call | tf_op jit(solution)/shard_map/while/body/eval_jaxpr/cond/branch_1_fun/vmap(jit(_cho_solve))/triangular_solve | solution.py:49
  78.1 69.0 %collective-permute-start.1 = (f32[1,2,128,128]{2,3,1,0:T(8,128)S(1)}, f32[1,2,128,128]{2,3,1,0:T(8,128)S(1)}, u32[]{:S(2)}, u32[]{:S(2)}) collective-permute-start(f32[1,2,128,128]{2,3,1,0:T(8,128)S(1)} %copy.33), channel_id=1, source_target_pairs={{0,1},{1,2},{2,3},{3,4},{4,5},{5,6},{6,7},{7,8},{8,9},{9,10},{10,1... | collective-permute-start | bytes 393224 | tf_op jit(solution)/shard_map/while/body/eval_jaxpr/ppermute | solution.py:17
  148.2 2.9 collective-permute-start.1
  152.2 72.1 %collective-permute-start.1 = (f32[1,2,128,128]{2,3,1,0:T(8,128)S(1)}, f32[1,2,128,128]{2,3,1,0:T(8,128)S(1)}, u32[]{:S(2)}, u32[]{:S(2)}) collective-permute-start(f32[1,2,128,128]{2,3,1,0:T(8,128)S(1)} %copy.33), channel_id=1, source_target_pairs={{0,1},{1,2},{2,3},{3,4},{4,5},{5,6},{6,7},{7,8},{8,9},{9,10},{10,1... | collective-permute-start | bytes 393224 | tf_op jit(solution)/shard_map/while/body/eval_jaxpr/ppermute | solution.py:17
  225.4 5.3 collective-permute-start.1
  231.7 65.6 %collective-permute-start.1 = (f32[1,2,128,128]{2,3,1,0:T(8,128)S(1)}, f32[1,2,128,128]{2,3,1,0:T(8,128)S(1)}, u32[]{:S(2)}, u32[]{:S(2)}) collective-permute-start(f32[1,2,128,128]{2,3,1,0:T(8,128)S(1)} %copy.33), channel_id=1, source_target_pairs={{0,1},{1,2},{2,3},{3,4},{4,5},{5,6},{6,7},{7,8},{8,9},{9,10},{10,1... | collective-permute-start | bytes 393224 | tf_op jit(solution)/shard_map/while/body/eval_jaxpr/ppermute | solution.py:17
  298.5 5.3 collective-permute-start.1
  304.8 69.6 %collective-permute-start.1 = (f32[1,2,128,128]{2,3,1,0:T(8,128)S(1)}, f32[1,2,128,128]{2,3,1,0:T(8,128)S(1)}, u32[]{:S(2)}, u32[]{:S(2)}) collective-permute-start(f32[1,2,128,128]{2,3,1,0:T(8,128)S(1)} %copy.33), channel_id=1, source_target_pairs={{0,1},{1,2},{2,3},{3,4},{4,5},{5,6},{6,7},{7,8},{8,9},{9,10},{10,1... | collective-permute-start | bytes 393224 | tf_op jit(solution)/shard_map/while/body/eval_jaxpr/ppermute | solution.py:17
  375.6 5.3 collective-permute-start.1
  382.0 65.6 %collective-permute-start.1 = (f32[1,2,128,128]{2,3,1,0:T(8,128)S(1)}, f32[1,2,128,128]{2,3,1,0:T(8,128)S(1)}, u32[]{:S(2)}, u32[]{:S(2)}) collective-permute-start(f32[1,2,128,128]{2,3,1,0:T(8,128)S(1)} %copy.33), channel_id=1, source_target_pairs={{0,1},{1,2},{2,3},{3,4},{4,5},{5,6},{6,7},{7,8},{8,9},{9,10},{10,1... | collective-permute-start | bytes 393224 | tf_op jit(solution)/shard_map/while/body/eval_jaxpr/ppermute | solution.py:17
  448.7 5.3 collective-permute-start.1
  455.0 69.6 %collective-permute-start.1 = (f32[1,2,128,128]{2,3,1,0:T(8,128)S(1)}, f32[1,2,128,128]{2,3,1,0:T(8,128)S(1)}, u32[]{:S(2)}, u32[]{:S(2)}) collective-permute-start(f32[1,2,128,128]{2,3,1,0:T(8,128)S(1)} %copy.33), channel_id=1, source_target_pairs={{0,1},{1,2},{2,3},{3,4},{4,5},{5,6},{6,7},{7,8},{8,9},{9,10},{10,1... | collective-permute-start | bytes 393224 | tf_op jit(solution)/shard_map/while/body/eval_jaxpr/ppermute | solution.py:17
  525.7 5.3 collective-permute-start.1
  532.1 65.6 %collective-permute-start.1 = (f32[1,2,128,128]{2,3,1,0:T(8,128)S(1)}, f32[1,2,128,128]{2,3,1,0:T(8,128)S(1)}, u32[]{:S(2)}, u32[]{:S(2)}) collective-permute-start(f32[1,2,128,128]{2,3,1,0:T(8,128)S(1)} %copy.33), channel_id=1, source_target_pairs={{0,1},{1,2},{2,3},{3,4},{4,5},{5,6},{6,7},{7,8},{8,9},{9,10},{10,1... | collective-permute-start | bytes 393224 | tf_op jit(solution)/shard_map/while/body/eval_jaxpr/ppermute | solution.py:17
  598.8 5.3 collective-permute-start.1
  605.9 699.7 %while.34 = (s32[]{:T(128)}, f32[1,1,256,256]{3,2,1,0:T(8,128)}, f32[1,2,128,128]{3,2,1,0:T(8,128)S(1)}, s32[]{:T(128)}, f32[1,1,256,256]{3,2,1,0:T(8,128)}, /*i...) while((s32[]{:T(128)}, f32[1,1,256,256]{3,2,1,0:T(8,128)}, f32[1,2,128,128]{3,2,1,0:T(8,128)S(1)}, ...), condition=%wide.region_11.12_spmd, body=%wide.region_8.11_spmd.sunk | while | flops 805617664 | bytes 4784343 | solution.py:162
  607.2 70.4 %collective-permute-done = f32[1,2,128,128]{3,2,1,0:T(8,128)S(1)} collective-permute-done((f32[1,2,128,128]{3,2,1,0:T(8,128)S(1)}, f32[1,2,128,128]{3,2,1,0:T(8,128)S(1)}, u32[]{:S(2)}, u32[]{:S(2)}) %collective-permute-start) | collective-permute-done | bytes 131104 | tf_op jit(solution)/shard_map/while/body/eval_jaxpr/ppermute | solution.py:17
  678.8 6.9 collective-permute-done
  687.0 64.0 %collective-permute-done = f32[1,2,128,128]{3,2,1,0:T(8,128)S(1)} collective-permute-done((f32[1,2,128,128]{3,2,1,0:T(8,128)S(1)}, f32[1,2,128,128]{3,2,1,0:T(8,128)S(1)}, u32[]{:S(2)}, u32[]{:S(2)}) %collective-permute-start) | collective-permute-done | bytes 131104 | tf_op jit(solution)/shard_map/while/body/eval_jaxpr/ppermute | solution.py:17
  752.3 6.9 collective-permute-done
  760.5 68.0 %collective-permute-done = f32[1,2,128,128]{3,2,1,0:T(8,128)S(1)} collective-permute-done((f32[1,2,128,128]{3,2,1,0:T(8,128)S(1)}, f32[1,2,128,128]{3,2,1,0:T(8,128)S(1)}, u32[]{:S(2)}, u32[]{:S(2)}) %collective-permute-start) | collective-permute-done | bytes 131104 | tf_op jit(solution)/shard_map/while/body/eval_jaxpr/ppermute | solution.py:17
  829.7 6.9 collective-permute-done
  837.9 64.0 %collective-permute-done = f32[1,2,128,128]{3,2,1,0:T(8,128)S(1)} collective-permute-done((f32[1,2,128,128]{3,2,1,0:T(8,128)S(1)}, f32[1,2,128,128]{3,2,1,0:T(8,128)S(1)}, u32[]{:S(2)}, u32[]{:S(2)}) %collective-permute-start) | collective-permute-done | bytes 131104 | tf_op jit(solution)/shard_map/while/body/eval_jaxpr/ppermute | solution.py:17
  903.2 6.9 collective-permute-done
  911.4 68.0 %collective-permute-done = f32[1,2,128,128]{3,2,1,0:T(8,128)S(1)} collective-permute-done((f32[1,2,128,128]{3,2,1,0:T(8,128)S(1)}, f32[1,2,128,128]{3,2,1,0:T(8,128)S(1)}, u32[]{:S(2)}, u32[]{:S(2)}) %collective-permute-start) | collective-permute-done | bytes 131104 | tf_op jit(solution)/shard_map/while/body/eval_jaxpr/ppermute | solution.py:17
  980.6 6.2 collective-permute-done
  988.1 64.7 %collective-permute-done = f32[1,2,128,128]{3,2,1,0:T(8,128)S(1)} collective-permute-done((f32[1,2,128,128]{3,2,1,0:T(8,128)S(1)}, f32[1,2,128,128]{3,2,1,0:T(8,128)S(1)}, u32[]{:S(2)}, u32[]{:S(2)}) %collective-permute-start) | collective-permute-done | bytes 131104 | tf_op jit(solution)/shard_map/while/body/eval_jaxpr/ppermute | solution.py:17
  1054.1 6.2 collective-permute-done
  1061.6 68.7 %collective-permute-done = f32[1,2,128,128]{3,2,1,0:T(8,128)S(1)} collective-permute-done((f32[1,2,128,128]{3,2,1,0:T(8,128)S(1)}, f32[1,2,128,128]{3,2,1,0:T(8,128)S(1)}, u32[]{:S(2)}, u32[]{:S(2)}) %collective-permute-start) | collective-permute-done | bytes 131104 | tf_op jit(solution)/shard_map/while/body/eval_jaxpr/ppermute | solution.py:17
  1131.5 6.2 collective-permute-done
  1139.0 64.2 %collective-permute-done = f32[1,2,128,128]{3,2,1,0:T(8,128)S(1)} collective-permute-done((f32[1,2,128,128]{3,2,1,0:T(8,128)S(1)}, f32[1,2,128,128]{3,2,1,0:T(8,128)S(1)}, u32[]{:S(2)}, u32[]{:S(2)}) %collective-permute-start) | collective-permute-done | bytes 131104 | tf_op jit(solution)/shard_map/while/body/eval_jaxpr/ppermute | solution.py:17
  1204.5 94.8 %collective-permute-done = f32[1,2,128,128]{3,2,1,0:T(8,128)S(1)} collective-permute-done((f32[1,2,128,128]{3,2,1,0:T(8,128)S(1)}, f32[1,2,128,128]{3,2,1,0:T(8,128)S(1)}, u32[]{:S(2)}, u32[]{:S(2)}) %collective-permute-start) | collective-permute-done | bytes 131104 | tf_op jit(solution)/shard_map/while/body/eval_jaxpr/ppermute | solution.py:17
  1299.4 6.2 conditional.6
  1306.5 45.5 %gather_fusion.2 = f32[8192]{0:T(1024)S(1)} fusion(f32[16384]{0:T(1024)S(1)} %get-tuple-element.437, s32[8192]{0:T(1024)S(1)} %broadcast_clamp_fusion), kind=kCustom, calls=%fused_computation.2.clone | custom fusion | bytes 98304 | tf_op jit(solution)/shard_map/jit(take_along_axis)/gather | solution.py:176
  1352.0 45.5 %gather_fusion = f32[8192]{0:T(1024)S(1)} fusion(f32[16384]{0:T(1024)S(1)} %get-tuple-element.437, s32[8192]{0:T(1024)S(1)} %broadcast_clamp_fusion.1), kind=kCustom, calls=%fused_computation.clone | custom fusion | bytes 98304 | tf_op jit(solution)/shard_map/jit(take_along_axis)/gather | solution.py:174
  1397.6 45.5 %gather_fusion.1 = f32[8192]{0:T(1024)S(1)} fusion(f32[16384]{0:T(1024)S(1)} %get-tuple-element.438, s32[8192]{0:T(1024)S(1)} %broadcast_clamp_fusion.1), kind=kCustom, calls=%fused_computation.1.clone | custom fusion | bytes 98304 | tf_op jit(solution)/shard_map/jit(take_along_axis)/gather | solution.py:175
  1443.1 45.5 %gather_fusion.3 = f32[8192]{0:T(1024)S(1)} fusion(f32[16384]{0:T(1024)S(1)} %get-tuple-element.438, s32[8192]{0:T(1024)S(1)} %broadcast_clamp_fusion), kind=kCustom, calls=%fused_computation.3.clone | custom fusion | bytes 98304 | tf_op jit(solution)/shard_map/jit(take_along_axis)/gather | solution.py:177
  1489.2 6.4 copy.27
  1496.1 38.4 %reduce.18 = f32[8192,4]{1,0:T(8,128)} reduce(f32[8192,1,1,4]{3,2,1,0:T(1,128)} %bitcast.248, f32[]{:T(128)} %broadcast.229), dimensions={1,2}, to_apply=%bitcast.209.reduce_sub_computation | reduce | bytes 262148
  1534.5 5.0 reshape.356
  1539.5 19.5 %all_to_all.18 = f32[32,1,1024]{2,1,0:T(1,128)S(1)} all-to-all(f32[32,1,1024]{2,1,0:T(1,128)S(1)} %reshape.356), channel_id=1, replica_groups=mesh['energy'=32,'chain'=16] {'energy'}, dimensions={0} | all-to-all | bytes 262144 | tf_op jit(solution)/shard_map/all_to_all | solution.py:181
  1560.0 8.0 reshape.357
  (182 shorter events, 74.7 us)
Async XLA Ops:
  6.2 2.7 collective-permute-start.1
  75.8 2.3 collective-permute-start.1
  78.1 70.0 %collective-permute-start.1 = (f32[1,2,128,128]{2,3,1,0:T(8,128)S(1)}, f32[1,2,128,128]{2,3,1,0:T(8,128)S(1)}, u32[]{:S(2)}, u32[]{:S(2)}) collective-permute-start(f32[1,2,128,128]{2,3,1,0:T(8,128)S(1)} %copy.33), channel_id=1, source_target_pairs={{0,1},{1,2},{2,3},{3,4},{4,5},{5,6},{6,7},{7,8},{8,9},{9,10},{10,1... | collective-permute-start | bytes 393224 | tf_op jit(solution)/shard_map/while/body/eval_jaxpr/ppermute | solution.py:17
  148.2 3.9 collective-permute-start.1
  152.2 73.1 %collective-permute-start.1 = (f32[1,2,128,128]{2,3,1,0:T(8,128)S(1)}, f32[1,2,128,128]{2,3,1,0:T(8,128)S(1)}, u32[]{:S(2)}, u32[]{:S(2)}) collective-permute-start(f32[1,2,128,128]{2,3,1,0:T(8,128)S(1)} %copy.33), channel_id=1, source_target_pairs={{0,1},{1,2},{2,3},{3,4},{4,5},{5,6},{6,7},{7,8},{8,9},{9,10},{10,1... | collective-permute-start | bytes 393224 | tf_op jit(solution)/shard_map/while/body/eval_jaxpr/ppermute | solution.py:17
  225.4 6.3 collective-permute-start.1
  231.7 66.6 %collective-permute-start.1 = (f32[1,2,128,128]{2,3,1,0:T(8,128)S(1)}, f32[1,2,128,128]{2,3,1,0:T(8,128)S(1)}, u32[]{:S(2)}, u32[]{:S(2)}) collective-permute-start(f32[1,2,128,128]{2,3,1,0:T(8,128)S(1)} %copy.33), channel_id=1, source_target_pairs={{0,1},{1,2},{2,3},{3,4},{4,5},{5,6},{6,7},{7,8},{8,9},{9,10},{10,1... | collective-permute-start | bytes 393224 | tf_op jit(solution)/shard_map/while/body/eval_jaxpr/ppermute | solution.py:17
  298.5 6.3 collective-permute-start.1
  304.8 70.6 %collective-permute-start.1 = (f32[1,2,128,128]{2,3,1,0:T(8,128)S(1)}, f32[1,2,128,128]{2,3,1,0:T(8,128)S(1)}, u32[]{:S(2)}, u32[]{:S(2)}) collective-permute-start(f32[1,2,128,128]{2,3,1,0:T(8,128)S(1)} %copy.33), channel_id=1, source_target_pairs={{0,1},{1,2},{2,3},{3,4},{4,5},{5,6},{6,7},{7,8},{8,9},{9,10},{10,1... | collective-permute-start | bytes 393224 | tf_op jit(solution)/shard_map/while/body/eval_jaxpr/ppermute | solution.py:17
  375.6 6.3 collective-permute-start.1
  382.0 66.6 %collective-permute-start.1 = (f32[1,2,128,128]{2,3,1,0:T(8,128)S(1)}, f32[1,2,128,128]{2,3,1,0:T(8,128)S(1)}, u32[]{:S(2)}, u32[]{:S(2)}) collective-permute-start(f32[1,2,128,128]{2,3,1,0:T(8,128)S(1)} %copy.33), channel_id=1, source_target_pairs={{0,1},{1,2},{2,3},{3,4},{4,5},{5,6},{6,7},{7,8},{8,9},{9,10},{10,1... | collective-permute-start | bytes 393224 | tf_op jit(solution)/shard_map/while/body/eval_jaxpr/ppermute | solution.py:17
  448.7 6.3 collective-permute-start.1
  455.0 70.6 %collective-permute-start.1 = (f32[1,2,128,128]{2,3,1,0:T(8,128)S(1)}, f32[1,2,128,128]{2,3,1,0:T(8,128)S(1)}, u32[]{:S(2)}, u32[]{:S(2)}) collective-permute-start(f32[1,2,128,128]{2,3,1,0:T(8,128)S(1)} %copy.33), channel_id=1, source_target_pairs={{0,1},{1,2},{2,3},{3,4},{4,5},{5,6},{6,7},{7,8},{8,9},{9,10},{10,1... | collective-permute-start | bytes 393224 | tf_op jit(solution)/shard_map/while/body/eval_jaxpr/ppermute | solution.py:17
  525.7 6.3 collective-permute-start.1
  532.1 66.6 %collective-permute-start.1 = (f32[1,2,128,128]{2,3,1,0:T(8,128)S(1)}, f32[1,2,128,128]{2,3,1,0:T(8,128)S(1)}, u32[]{:S(2)}, u32[]{:S(2)}) collective-permute-start(f32[1,2,128,128]{2,3,1,0:T(8,128)S(1)} %copy.33), channel_id=1, source_target_pairs={{0,1},{1,2},{2,3},{3,4},{4,5},{5,6},{6,7},{7,8},{8,9},{9,10},{10,1... | collective-permute-start | bytes 393224 | tf_op jit(solution)/shard_map/while/body/eval_jaxpr/ppermute | solution.py:17
  598.8 6.3 collective-permute-start.1
  605.9 71.7 %collective-permute-start = (f32[1,2,128,128]{3,2,1,0:T(8,128)S(1)}, f32[1,2,128,128]{3,2,1,0:T(8,128)S(1)}, u32[]{:S(2)}, u32[]{:S(2)}) collective-permute-start(f32[1,2,128,128]{3,2,1,0:T(8,128)S(1)} %get-tuple-element.638), channel_id=1, source_target_pairs={{1,0},{2,1},{3,2},{4,3},{5,4},{6,5},{7,6},{8,7},{9,8},{10,9},{11,1... | collective-permute-start | bytes 393224 | tf_op jit(solution)/shard_map/while/body/eval_jaxpr/ppermute | solution.py:17
  677.5 8.2 collective-permute-start
  685.7 65.3 %collective-permute-start = (f32[1,2,128,128]{3,2,1,0:T(8,128)S(1)}, f32[1,2,128,128]{3,2,1,0:T(8,128)S(1)}, u32[]{:S(2)}, u32[]{:S(2)}) collective-permute-start(f32[1,2,128,128]{3,2,1,0:T(8,128)S(1)} %get-tuple-element.638), channel_id=1, source_target_pairs={{1,0},{2,1},{3,2},{4,3},{5,4},{6,5},{7,6},{8,7},{9,8},{10,9},{11,1... | collective-permute-start | bytes 393224 | tf_op jit(solution)/shard_map/while/body/eval_jaxpr/ppermute | solution.py:17
  751.0 8.2 collective-permute-start
  759.2 69.3 %collective-permute-start = (f32[1,2,128,128]{3,2,1,0:T(8,128)S(1)}, f32[1,2,128,128]{3,2,1,0:T(8,128)S(1)}, u32[]{:S(2)}, u32[]{:S(2)}) collective-permute-start(f32[1,2,128,128]{3,2,1,0:T(8,128)S(1)} %get-tuple-element.638), channel_id=1, source_target_pairs={{1,0},{2,1},{3,2},{4,3},{5,4},{6,5},{7,6},{8,7},{9,8},{10,9},{11,1... | collective-permute-start | bytes 393224 | tf_op jit(solution)/shard_map/while/body/eval_jaxpr/ppermute | solution.py:17
  828.4 8.2 collective-permute-start
  836.6 65.2 %collective-permute-start = (f32[1,2,128,128]{3,2,1,0:T(8,128)S(1)}, f32[1,2,128,128]{3,2,1,0:T(8,128)S(1)}, u32[]{:S(2)}, u32[]{:S(2)}) collective-permute-start(f32[1,2,128,128]{3,2,1,0:T(8,128)S(1)} %get-tuple-element.638), channel_id=1, source_target_pairs={{1,0},{2,1},{3,2},{4,3},{5,4},{6,5},{7,6},{8,7},{9,8},{10,9},{11,1... | collective-permute-start | bytes 393224 | tf_op jit(solution)/shard_map/while/body/eval_jaxpr/ppermute | solution.py:17
  901.9 8.2 collective-permute-start
  910.1 69.3 %collective-permute-start = (f32[1,2,128,128]{3,2,1,0:T(8,128)S(1)}, f32[1,2,128,128]{3,2,1,0:T(8,128)S(1)}, u32[]{:S(2)}, u32[]{:S(2)}) collective-permute-start(f32[1,2,128,128]{3,2,1,0:T(8,128)S(1)} %get-tuple-element.638), channel_id=1, source_target_pairs={{1,0},{2,1},{3,2},{4,3},{5,4},{6,5},{7,6},{8,7},{9,8},{10,9},{11,1... | collective-permute-start | bytes 393224 | tf_op jit(solution)/shard_map/while/body/eval_jaxpr/ppermute | solution.py:17
  979.4 7.5 collective-permute-start
  986.8 66.0 %collective-permute-start = (f32[1,2,128,128]{3,2,1,0:T(8,128)S(1)}, f32[1,2,128,128]{3,2,1,0:T(8,128)S(1)}, u32[]{:S(2)}, u32[]{:S(2)}) collective-permute-start(f32[1,2,128,128]{3,2,1,0:T(8,128)S(1)} %get-tuple-element.638), channel_id=1, source_target_pairs={{1,0},{2,1},{3,2},{4,3},{5,4},{6,5},{7,6},{8,7},{9,8},{10,9},{11,1... | collective-permute-start | bytes 393224 | tf_op jit(solution)/shard_map/while/body/eval_jaxpr/ppermute | solution.py:17
  1052.8 7.5 collective-permute-start
  1060.3 69.9 %collective-permute-start = (f32[1,2,128,128]{3,2,1,0:T(8,128)S(1)}, f32[1,2,128,128]{3,2,1,0:T(8,128)S(1)}, u32[]{:S(2)}, u32[]{:S(2)}) collective-permute-start(f32[1,2,128,128]{3,2,1,0:T(8,128)S(1)} %get-tuple-element.638), channel_id=1, source_target_pairs={{1,0},{2,1},{3,2},{4,3},{5,4},{6,5},{7,6},{8,7},{9,8},{10,9},{11,1... | collective-permute-start | bytes 393224 | tf_op jit(solution)/shard_map/while/body/eval_jaxpr/ppermute | solution.py:17
  1130.2 7.5 collective-permute-start
  1137.7 65.5 %collective-permute-start = (f32[1,2,128,128]{3,2,1,0:T(8,128)S(1)}, f32[1,2,128,128]{3,2,1,0:T(8,128)S(1)}, u32[]{:S(2)}, u32[]{:S(2)}) collective-permute-start(f32[1,2,128,128]{3,2,1,0:T(8,128)S(1)} %get-tuple-element.638), channel_id=1, source_target_pairs={{1,0},{2,1},{3,2},{4,3},{5,4},{6,5},{7,6},{8,7},{9,8},{10,9},{11,1... | collective-permute-start | bytes 393224 | tf_op jit(solution)/shard_map/while/body/eval_jaxpr/ppermute | solution.py:17
  1203.2 96.1 %collective-permute-start = (f32[1,2,128,128]{3,2,1,0:T(8,128)S(1)}, f32[1,2,128,128]{3,2,1,0:T(8,128)S(1)}, u32[]{:S(2)}, u32[]{:S(2)}) collective-permute-start(f32[1,2,128,128]{3,2,1,0:T(8,128)S(1)} %get-tuple-element.638), channel_id=1, source_target_pairs={{1,0},{2,1},{3,2},{4,3},{5,4},{6,5},{7,6},{8,7},{9,8},{10,9},{11,1... | collective-permute-start | bytes 393224 | tf_op jit(solution)/shard_map/while/body/eval_jaxpr/ppermute | solution.py:17
  1443.1 45.6 %copy-start = (s32[1,8192]{1,0:T(1,128)S(1)}, s32[1,8192]{1,0:T(1,128)}, u32[]{:S(2)}) copy-start(s32[1,8192]{1,0:T(1,128)} %param.15) | copy-start | bytes 98308
where the time goes:
time: 1580 us; the launch traced here: 1570 us
  waiting for transfers between devices  688 us (44%)
  starting transfers between devices  536 us (34%)
  local copies, waits for them, and re-layouts  217 us (14%)
  other arithmetic  97.4 us (6%)
  blocking collectives  19.5 us (1%)
    ppermute x32, waiting for transfers between devices, shifted_2(): return lax.ppermute(value, axis, pairs)  688 us
    ppermute x32, starting transfers between devices, shifted_2(): return lax.ppermute(value, axis, pairs)  536 us
    gather x1, local copies, waits for them, and re-layouts, shards(): jnp.take_along_axis(real_flat, mirror_index, axis=2)  45.5 us
    gather x1, local copies, waits for them, and re-layouts, shards(): jnp.take_along_axis(imag_flat, mirror_index, axis=2)  45.5 us
    gather x1, local copies, waits for them, and re-layouts, shards(): jnp.take_along_axis(real_flat, direct_index, axis=2)  45.5 us
    gather x1, local copies, waits for them, and re-layouts, shards(): jnp.take_along_axis(imag_flat, direct_index, axis=2)  45.5 us
    unnamed x1, other arithmetic  38.4 us
    another operation x7, other arithmetic, invert(): factor = jnp.linalg.cholesky(normal)  34.7 us
  transfers between devices with their start and end apart: 32, of which 32 were waited for; matrix products, arithmetic and copies ran while one was open for 0% of the time, Pallas kernels for 0%

commit v1 on v0

v1 whole, which is shorter than its diff:
```python
import jax
import jax.numpy as jnp
from jax import lax
from jax.experimental import pallas as pl
from jax.experimental.pallas import tpu as pltpu
from jax.sharding import PartitionSpec as P

ORB = 128
BROADENING = 0.04
PANEL = 32
F32 = jnp.float32
CHAINS = 16


def product(left, right):
    return jnp.dot(left, right, precision=lax.Precision.HIGHEST, preferred_element_type=F32)


def rep(packed):
    real, imag = packed[:, :ORB], packed[:, ORB:]
    upper = jnp.concatenate([real, imag], axis=1)
    lower = jnp.concatenate([-imag, real], axis=1)
    return jnp.concatenate([upper, lower], axis=0)


def adjoint(packed):
    return jnp.concatenate([packed[:, :ORB].T, -packed[:, ORB:].T], axis=1)


def cmul(ar, ai, br, bi):
    return ar * br - ai * bi, ar * bi + ai * br


def lanes(x, j):
    return jnp.broadcast_to(x[..., j : j + 1], x.shape)


def sublanes(x3, k):
    tile = x3[k // 8]
    return jnp.take_along_axis(tile, jnp.full((8, 128), k % 8, jnp.int32), axis=0)


def panel_step(xr, xi, off):
    nb = xr.shape[0]
    shape = (nb, 8, 128)
    row = lax.broadcasted_iota(jnp.int32, shape, 0) * 8 + lax.broadcasted_iota(jnp.int32, shape, 1)
    lane = lax.broadcasted_iota(jnp.int32, shape, 2)
    lane1 = lane[0]
    for k in range(0, nb * 8, 2):
        j = off + k
        c0r, c0i, c1r, c1i = lanes(xr, j), lanes(xi, j), lanes(xr, j + 1), lanes(xi, j + 1)
        r0r, r0i = sublanes(xr, k), sublanes(xi, k)
        r1r, r1i = sublanes(xr, k + 1), sublanes(xi, k + 1)
        pr, pi = sublanes(c0r, k), sublanes(c0i, k)
        qr, qi = sublanes(c1r, k), sublanes(c1i, k)
        tr, ti = sublanes(c0r, k + 1), sublanes(c0i, k + 1)
        ur, ui = sublanes(c1r, k + 1), sublanes(c1i, k + 1)
        dr, di = cmul(pr, pi, ur, ui)
        er, ei = cmul(qr, qi, tr, ti)
        dr, di = dr - er, di - ei
        d = 1.0 / (dr * dr + di * di)
        m0, m1 = lane1 == j, lane1 == j + 1
        mm = m0 | m1
        r0r = jnp.where(m0, 1.0, jnp.where(m1, 0.0, r0r))
        r0i = jnp.where(mm, 0.0, r0i)
        r1r = jnp.where(m1, 1.0, jnp.where(m0, 0.0, r1r))
        r1i = jnp.where(mm, 0.0, r1i)
        ar, ai = cmul(ur, ui, r0r, r0i)
        br, bi = cmul(qr, qi, r1r, r1i)
        s0r, s0i = cmul(ar - br, ai - bi, dr, -di)
        ar, ai = cmul(pr, pi, r1r, r1i)
        br, bi = cmul(tr, ti, r0r, r0i)
        s1r, s1i = cmul(ar - br, ai - bi, dr, -di)
        k0, k1 = row == k, row == k + 1
        kk = k0 | k1
        z = kk | (lane == j) | (lane == j + 1)
        c0r = jnp.where(k0, -1.0, jnp.where(k1, 0.0, c0r))
        c0i = jnp.where(kk, 0.0, c0i)
        c1r = jnp.where(k1, -1.0, jnp.where(k0, 0.0, c1r))
        c1i = jnp.where(kk, 0.0, c1i)
        e0r, e0i = cmul(c0r, c0i, s0r, s0i)
        e1r, e1i = cmul(c1r, c1i, s1r, s1i)
        xr = jnp.where(z, 0.0, xr) - (e0r + e1r) * d
        xi = jnp.where(z, 0.0, xi) - (e0i + e1i) * d
    return xr, xi


def invert(packed, ar, ai):
    ar[...] = packed[:, :ORB]
    ai[...] = packed[:, ORB:]
    b = PANEL
    count = ORB // b
    lane = lax.broadcasted_iota(jnp.int32, (b, ORB), 1)
    for t in range(count):
        s = slice(t * b, (t + 1) * b)
        shape = (b // 8, 8, 128)
        xr, xi = panel_step(ar[s, :].reshape(shape), ai[s, :].reshape(shape), t * b)
        xr, xi = xr.reshape(b, ORB), xi.reshape(b, ORB)
        table = rep(jnp.concatenate([xr, xi], axis=1))
        inside = (lane >= t * b) & (lane < (t + 1) * b)
        for q in range(1, count):
            u = (t + q) % count
            other = slice(u * b, (u + 1) * b)
            column = jnp.concatenate([ar[other, s], ai[other, s]], axis=1)
            delta = product(column, table)
            ar[other, :] = jnp.where(inside, 0.0, ar[other, :]) - delta[:, :ORB]
            ai[other, :] = jnp.where(inside, 0.0, ai[other, :]) - delta[:, ORB:]
        ar[s, :] = xr
        ai[s, :] = xi
    return jnp.concatenate([ar[...], ai[...]], axis=1)


SCRATCH = [pltpu.VMEM((ORB, ORB), F32), pltpu.VMEM((ORB, ORB), F32)]
PACKED = jax.ShapeDtypeStruct((ORB, 2 * ORB), F32)
DOUBLE = jax.ShapeDtypeStruct((ORB, 4 * ORB), F32)
VM = pl.BlockSpec(memory_space=pltpu.VMEM)
SM = pl.BlockSpec(memory_space=pltpu.SMEM)


def first_kernel(scalars, onsite, coupling, diag_out, inverse_out, coupler_out, ar, ai):
    energy = scalars[0]
    last = scalars[1]
    row = lax.broadcasted_iota(jnp.int32, (ORB, ORB), 0)
    column = lax.broadcasted_iota(jnp.int32, (ORB, ORB), 1)
    eye = row == column
    raw_real, raw_imag = onsite[0, 0], onsite[0, 1]
    real = jnp.where(eye, energy, 0.0) - 0.5 * (raw_real + raw_real.T)
    imag = jnp.where(eye, BROADENING, 0.0) - 0.5 * (raw_imag - raw_imag.T)
    coupler = jnp.concatenate([coupling[0, 0], coupling[0, 1]], axis=1)
    diag_out[...] = jnp.concatenate([real, imag], axis=1)
    coupler_out[...] = -coupler

    @pl.when(last > 0.5)
    def contact():
        square = product(coupler, rep(adjoint(coupler)))
        diag_out[:, :ORB] = real - 0.5 * square[:, ORB:]
        diag_out[:, ORB:] = imag + 0.5 * square[:, :ORB]
        coupler_out[...] = jnp.zeros_like(coupler)

    inverse_out[...] = invert(diag_out[...], ar, ai)


def second_kernel(inverse, upper, previous, lower_out, send_out):
    lower = -adjoint(jnp.concatenate([previous[0, 0], previous[0, 1]], axis=1))
    lower_out[...] = lower
    send_out[:, : 2 * ORB] = product(inverse[...], rep(upper[...]))
    send_out[:, 2 * ORB :] = product(inverse[...], rep(lower))


def level_kernel(diag, lower, upper, left, right, diag_out, lower_out, upper_out, send_out, ar, ai):
    from_left = product(lower[...], rep(left[:, : 2 * ORB]))
    from_right = product(upper[...], rep(right[:, 2 * ORB :]))
    new_diag = diag[...] - from_left - from_right
    diag_out[...] = new_diag
    new_lower = -product(lower[...], rep(left[:, 2 * ORB :]))
    new_upper = -product(upper[...], rep(right[:, : 2 * ORB]))
    lower_out[...] = new_lower
    upper_out[...] = new_upper
    inverse = invert(new_diag, ar, ai)
    send_out[:, : 2 * ORB] = product(inverse, rep(new_upper))
    send_out[:, 2 * ORB :] = product(inverse, rep(new_lower))


def fourth_kernel(diag, lower, upper, left, right, diag_out, across_out, send_out, ar, ai):
    from_left = product(lower[...], rep(left[:, : 2 * ORB]))
    from_right = product(upper[...], rep(right[:, 2 * ORB :]))
    new_diag = diag[...] - from_left - from_right
    diag_out[...] = new_diag
    new_lower = -product(lower[...], rep(left[:, 2 * ORB :]))
    new_upper = -product(upper[...], rep(right[:, : 2 * ORB]))
    across = new_lower + new_upper
    across_out[...] = across
    inverse = invert(new_diag, ar, ai)
    send_out[...] = product(inverse, rep(across))


def last_kernel(diag, across, partner, retained, out, ar, ai):
    green = invert(diag[...] - product(across[...], rep(partner[...])), ar, ai)
    turned = jnp.concatenate([green[:, :ORB].T, green[:, ORB:].T], axis=0)
    high = turned.astype(jnp.bfloat16)
    rest = turned - high.astype(F32)
    middle = rest.astype(jnp.bfloat16)
    table = jnp.concatenate([high, middle], axis=1)
    rows = lax.broadcasted_iota(jnp.int32, (ORB, 256), 0)

    def chunk(step, carry):
        index = retained[0:1, pl.ds(pl.multiple_of(step * 256, 256), 256)]
        first = rows == (index >> 7)
        second = rows == (index & 127)
        hot_first = jnp.where(first, 1.0, 0.0).astype(jnp.bfloat16)
        hot_second = jnp.where(second, 1.0, 0.0).astype(jnp.bfloat16)
        direct = jnp.dot(
            table, jnp.concatenate([hot_first, hot_first], axis=0), preferred_element_type=F32
        )
        mirror = jnp.dot(
            table, jnp.concatenate([hot_second, hot_second], axis=0), preferred_element_type=F32
        )
        parts = [
            jnp.where(second, direct[:ORB], 0.0),
            jnp.where(second, direct[ORB:], 0.0),
            jnp.where(first, mirror[:ORB], 0.0),
            jnp.where(first, mirror[ORB:], 0.0),
        ]
        sums = [jnp.sum(part, axis=0, keepdims=True) for part in parts]
        tile = []
        for value in sums:
            tile += [value[:, :128], value[:, 128:]]
        out[step] = jnp.concatenate(tile, axis=0)
        return carry

    lax.fori_loop(0, 32, chunk, 0)


def correlate_kernel(received, out, second_real, second_imag):
    for half in range(2):
        s = slice(half * 128, (half + 1) * 128)
        ar = received[pl.ds(0 + half, 32, stride=8), :]
        ai = received[pl.ds(2 + half, 32, stride=8), :]
        br = received[pl.ds(4 + half, 32, stride=8), :]
        bi = received[pl.ds(6 + half, 32, stride=8), :]
        second_real[0:32, :] = br
        second_real[32:64, :] = br
        second_imag[0:32, :] = bi
        second_imag[32:64, :] = bi
        total_real = jnp.zeros((32, 128), F32)
        total_imag = jnp.zeros((32, 128), F32)
        for n in range(32):
            xr = jnp.broadcast_to(ar[n : n + 1, :], (32, 128))
            xi = jnp.broadcast_to(ai[n : n + 1, :], (32, 128))
            yr = second_real[n : n + 32, :]
            yi = second_imag[n : n + 32, :]
            pr, pi = cmul(xr, xi, yr, yi)
            total_real += pr
            total_imag += pi
        out[0, :, s] = total_real
        out[1, :, s] = total_imag


def green_pairs(onsite, coupling, retained, energy):
    position = lax.axis_index("chain")
    scalars = jnp.stack([energy, (position == CHAINS - 1).astype(F32)])

    def moved(value, by):
        pairs = [(i, i + by) for i in range(CHAINS) if 0 <= i + by < CHAINS]
        return lax.ppermute(value, "chain", pairs)

    previous = moved(coupling, 1)
    diag, inverse, upper = pl.pallas_call(
        first_kernel,
        in_specs=[SM, VM, VM],
        out_shape=[PACKED, PACKED, PACKED],
        scratch_shapes=SCRATCH,
    )(scalars, onsite, coupling)
    lower, send = pl.pallas_call(second_kernel, out_shape=[PACKED, DOUBLE])(
        inverse, upper, previous
    )
    for distance in (1, 2):
        left = moved(send, distance)
        right = moved(send, -distance)
        diag, lower, upper, send = pl.pallas_call(
            level_kernel,
            out_shape=[PACKED, PACKED, PACKED, DOUBLE],
            scratch_shapes=SCRATCH,
        )(diag, lower, upper, left, right)
    left = moved(send, 4)
    right = moved(send, -4)
    diag, across, send = pl.pallas_call(
        fourth_kernel,
        out_shape=[PACKED, PACKED, PACKED],
        scratch_shapes=SCRATCH,
    )(diag, lower, upper, left, right)
    partner = lax.ppermute(send, "chain", [(i, (i + 8) % CHAINS) for i in range(CHAINS)])
    return pl.pallas_call(
        last_kernel,
        out_shape=jax.ShapeDtypeStruct((32, 8, 128), F32),
        scratch_shapes=SCRATCH,
    )(diag, across, partner, retained)


def correlate(received):
    result = pl.pallas_call(
        correlate_kernel,
        out_shape=jax.ShapeDtypeStruct((2, 32, 256), F32),
        scratch_shapes=[pltpu.VMEM((64, 128), F32), pltpu.VMEM((64, 128), F32)],
    )(received.reshape(256, 128))
    return result.reshape(2, 32, 1, 256)


def shards(onsite, coupling, retained):
    groups = lax.axis_size("energy")
    energy = -2.0 + 4.0 * lax.axis_index("energy").astype(F32) / groups
    gathered = green_pairs(onsite, coupling, retained, energy)
    received = lax.all_to_all(gathered, "energy", split_axis=0, concat_axis=0, tiled=True)
    return correlate(received)


def solution(mesh):
    in_specs = (P("chain", None, None, None), P("chain", None, None, None), P("chain", None))
    out_specs = P(None, None, "chain", "energy")
    return jax.shard_map(shards, mesh=mesh, in_specs=in_specs, out_specs=out_specs, check_vma=False)
```

time: 1580 us -> 146 us (0.09)
  waiting for transfers between devices: 688 us -> 21.6 us
  starting transfers between devices: 536 us -> 40.2 us
  local copies, waits for them, and re-layouts: 217 us -> 5.06 us
  other arithmetic: 97.4 us -> 0.67 us
  Pallas kernels: 0 us -> 57.7 us
    ppermute x32 -> x8, waiting for transfers between devices: 688 us -> 21.6 us  [the longest x7 18 us: moved(): return lax.ppermute(value, 'chain', pairs)]
    ppermute x32 -> x8, starting transfers between devices: 536 us -> 40.2 us  [the longest x7 26.5 us: moved(): return lax.ppermute(value, 'chain', pairs)]
    gather x4 -> x0, local copies, waits for them, and re-layouts: 182 us -> none  [the longest x1 45.5 us: shards(): jnp.take_along_axis(real_flat, mirror_index, axis=2)]
    pallas_call x0 -> x7, Pallas kernels: none -> 57.7 us  [the longest x2 18.8 us: green_pairs(): pl.pallas_call(level_kernel, out_shape=[PACKED, PACKED, PACKED, DOUBLE],...]
    another operation x12 -> x1, other arithmetic: 54.9 us -> 0.67 us  [green_pairs(): scalars = jnp.stack([energy, (position == CHAINS - 1).astype(F32)])]
    unnamed x1 -> x0, other arithmetic: 38.4 us -> none
  transfers between devices with their start and end apart: 32 -> 8, of which waited for: 32 -> 5; matrix products, arithmetic and copies ran while one was open for 0% -> 0% of each run, Pallas kernels for 0% -> 6%
where the time goes in v1:
time: 146 us; the launch traced here: 145 us
  Pallas kernels  57.7 us (40%)
  starting transfers between devices  40.2 us (28%)
  waiting for transfers between devices  21.6 us (15%)
  blocking collectives  19.8 us (14%)
  local copies, waits for them, and re-layouts  5.06 us (3%)
    ppermute x7, starting transfers between devices, moved(): return lax.ppermute(value, 'chain', pairs)  26.5 us
    all_to_all x1, blocking collectives, shards(): lax.all_to_all(gathered, 'energy', split_axis=0, concat_axis=0, tiled=True)  19.8 us
    pallas_call x2, Pallas kernels, green_pairs(): pl.pallas_call(level_kernel, out_shape=[PACKED, PACKED, PACKED, DOUBLE],...  18.8 us
    ppermute x7, waiting for transfers between devices, moved(): return lax.ppermute(value, 'chain', pairs)  18 us
    pallas_call x1, Pallas kernels, green_pairs(): pl.pallas_call(last_kernel, out_shape=jax.ShapeDtypeStruct((32, 8, 128),...  17 us
    ppermute x1, starting transfers between devices, green_pairs(): lax.ppermute(send, 'chain', [(i, (i + 8) % CHAINS) for i in range(CHAINS)])  13.7 us
    pallas_call x1, Pallas kernels, green_pairs(): pl.pallas_call(fourth_kernel, out_shape=[PACKED, PACKED, PACKED], scratch...  9.42 us
    pallas_call x1, Pallas kernels, green_pairs(): pl.pallas_call(first_kernel, in_specs=[SM, VM, VM], out_shape=[PACKED, PA...  8.54 us
  transfers between devices with their start and end apart: 8, of which 5 were waited for; matrix products, arithmetic and copies ran while one was open for 0% of the time, Pallas kernels for 6%

profile of v1, /device:TPU:8, one launch (start us, length us, event | category | flops | bytes accessed | tf_op | source)
XLA Modules:
  0.0 145.1 jit_solution(16576339708806734965)
XLA Ops:
  0.0 1.7 %collective-permute-start = (f32[1,2,128,128]{3,2,1,0:T(8,128)}, f32[1,2,128,128]{3,2,1,0:T(8,128)S(1)}, u32[]{:S(2)}, u32[]{:S(2)}) collective-permute-start(f32[1,2,128,128]{3,2,1,0:T(8,128)} %coupling.1), channel_id=1, source_target_pairs={{0,1},{1,2},{2,3},{3,4},{4,5},{5,6},{6,7},{7,8},{8,9},{9,10},{10,1... | collective-permute-start | bytes 393224 | tf_op jit(solution)/shard_map/ppermute | solution.py:245
  1.8 0.7 pad_maximum_fusion.scalars
  2.4 8.5 %shard_map.37 = (f32[128,256]{1,0:T(8,128)}, f32[128,256]{1,0:T(8,128)}, f32[128,256]{1,0:T(8,128)}) custom-call(f32[2]{0:T(128)} %pad_maximum_fusion.scalars, f32[1,2,128,128]{3,2,1,0:T(8,128)} %onsite.1, f32[1,2,128,128]{3,2,1,0:T(8,128)} %coupling.1), custom_call_target="tpu_custom_call" | custom-call | tf_op jit(solution)/shard_map/pallas_call | solution.py:248
  11.0 0.0 collective-permute-done.previous
  11.0 0.0 copy-start.6
  11.0 0.7 copy-done.6
  11.6 2.2 %shard_map.38 = (f32[128,256]{1,0:T(8,128)}, f32[128,512]{1,0:T(8,128)}) custom-call(f32[128,256]{1,0:T(8,128)} %get-tuple-element.22.inverse, f32[128,256]{1,0:T(8,128)} %get-tuple-element.23.upper, f32[1,2,128,128]{3,2,1,0:T(8,128)} %copy-done.6), custom_call_target="tpu_custom_call" | custom-call | tf_op jit(solution)/shard_map/pallas_call | solution.py:254
  13.8 1.3 collective-permute-start.2
  15.1 5.2 %collective-permute-start.1 = (f32[128,512]{1,0:T(8,128)}, f32[128,512]{1,0:T(8,128)S(1)}, u32[]{:S(2)}, u32[]{:S(2)}) collective-permute-start(f32[128,512]{1,0:T(8,128)} %get-tuple-element.25), channel_id=1, source_target_pairs={{0,1},{1,2},{2,3},{3,4},{4,5},{5,6},{6,7},{7,8},{8,9},{9,10},{10,1... | collective-permute-start | bytes 786440 | tf_op jit(solution)/shard_map/ppermute | solution.py:245
  20.3 0.0 collective-permute-done.2.right
  20.3 0.0 copy-start
  20.3 1.3 collective-permute-done.1.left
  21.6 0.0 copy-start.3
  21.6 0.0 copy-done
  21.6 0.7 copy-done.3
  22.3 9.4 %shard_map.39 = (f32[128,256]{1,0:T(8,128)}, f32[128,256]{1,0:T(8,128)}, f32[128,256]{1,0:T(8,128)}, f32[128,512]{1,0:T(8,128)}) custom-call(f32[128,256]{1,0:T(8,128)} %get-tuple-element.21.diag, f32[128,256]{1,0:T(8,128)} %get-tuple-element.24.lower, f32[128,256]{1,0:T(8,128)} %get-tuple-element.23.upper, f32[128,512]{1,0:T(8,128)} %copy-done.3, ...), custom_call_target="tpu_custom_call" | custom-call | tf_op jit(solution)/shard_map/pallas_call | solution.py:260
  31.8 1.3 collective-permute-start.4
  33.0 9.0 %collective-permute-start.3 = (f32[128,512]{1,0:T(8,128)}, f32[128,512]{1,0:T(8,128)S(1)}, u32[]{:S(2)}, u32[]{:S(2)}) collective-permute-start(f32[128,512]{1,0:T(8,128)} %get-tuple-element.29), channel_id=1, source_target_pairs={{0,2},{1,3},{2,4},{3,5},{4,6},{5,7},{6,8},{7,9},{8,10},{9,11},{10,... | collective-permute-start | bytes 786440 | tf_op jit(solution)/shard_map/ppermute | solution.py:245
  42.0 4.7 %collective-permute-done.4.right = f32[128,512]{1,0:T(8,128)S(1)} collective-permute-done((f32[128,512]{1,0:T(8,128)}, f32[128,512]{1,0:T(8,128)S(1)}, u32[]{:S(2)}, u32[]{:S(2)}) %collective-permute-start.4) | collective-permute-done | bytes 262176 | tf_op jit(solution)/shard_map/ppermute | solution.py:245
  46.7 0.0 copy-start.1
  46.7 1.3 collective-permute-done.3.left
  48.0 0.0 copy-start.4
  48.0 0.0 copy-done.1
  48.0 0.7 copy-done.4
  48.7 9.4 %shard_map.40 = (f32[128,256]{1,0:T(8,128)}, f32[128,256]{1,0:T(8,128)}, f32[128,256]{1,0:T(8,128)}, f32[128,512]{1,0:T(8,128)}) custom-call(f32[128,256]{1,0:T(8,128)} %get-tuple-element.26.diag, f32[128,256]{1,0:T(8,128)} %get-tuple-element.27.lower, f32[128,256]{1,0:T(8,128)} %get-tuple-element.28.upper, f32[128,512]{1,0:T(8,128)} %copy-done.4, ...), custom_call_target="tpu_custom_call" | custom-call | tf_op jit(solution)/shard_map/pallas_call | solution.py:260
  58.1 1.3 collective-permute-start.6
  59.4 6.7 %collective-permute-start.5 = (f32[128,512]{1,0:T(8,128)}, f32[128,512]{1,0:T(8,128)S(1)}, u32[]{:S(2)}, u32[]{:S(2)}) collective-permute-start(f32[128,512]{1,0:T(8,128)} %get-tuple-element.33), channel_id=1, source_target_pairs={{0,4},{1,5},{2,6},{3,7},{4,8},{5,9},{6,10},{7,11},{8,12},{9,13},{1... | collective-permute-start | bytes 786440 | tf_op jit(solution)/shard_map/ppermute | solution.py:245
  66.1 10.7 %collective-permute-done.6.right = f32[128,512]{1,0:T(8,128)S(1)} collective-permute-done((f32[128,512]{1,0:T(8,128)}, f32[128,512]{1,0:T(8,128)S(1)}, u32[]{:S(2)}, u32[]{:S(2)}) %collective-permute-start.6) | collective-permute-done | bytes 262176 | tf_op jit(solution)/shard_map/ppermute | solution.py:245
  76.9 0.0 copy-start.2
  76.9 0.0 collective-permute-done.5.left
  76.9 0.0 copy-start.5
  76.9 0.7 copy-done.2
  77.6 0.1 copy-done.5
  77.7 9.4 %shard_map.41 = (f32[128,256]{1,0:T(8,128)}, f32[128,256]{1,0:T(8,128)}, f32[128,256]{1,0:T(8,128)}) custom-call(f32[128,256]{1,0:T(8,128)} %get-tuple-element.30.diag, f32[128,256]{1,0:T(8,128)} %get-tuple-element.31.lower, f32[128,256]{1,0:T(8,128)} %get-tuple-element.32.upper, f32[128,512]{1,0:T(8,128)} %copy-done.5, f32[128,512]{1,0:T(8,128)} %copy-done.2), custom_call_target="tpu_custom_call" | custom-call | tf_op jit(solution)/shard_map/pallas_call | solution.py:267
  87.1 13.7 %collective-permute-start.7 = (f32[128,256]{1,0:T(8,128)}, f32[128,256]{1,0:T(8,128)S(1)}, u32[]{:S(2)}, u32[]{:S(2)}) collective-permute-start(f32[128,256]{1,0:T(8,128)} %get-tuple-element.36), channel_id=1, source_target_pairs={{0,8},{1,9},{2,10},{3,11},{4,12},{5,13},{6,14},{7,15},{8,0},{9,1},... | collective-permute-start | bytes 393224 | tf_op jit(solution)/shard_map/ppermute | solution.py:272
  100.8 3.5 %collective-permute-done.7.partner = f32[128,256]{1,0:T(8,128)S(1)} collective-permute-done((f32[128,256]{1,0:T(8,128)}, f32[128,256]{1,0:T(8,128)S(1)}, u32[]{:S(2)}, u32[]{:S(2)}) %collective-permute-start.7) | collective-permute-done | bytes 131104 | tf_op jit(solution)/shard_map/ppermute | solution.py:272
  104.3 0.0 copy-start.7
  104.3 0.7 copy-done.7
  105.0 17.0 %shard_map.42 = f32[32,8,128]{2,1,0:T(8,128)} custom-call(f32[128,256]{1,0:T(8,128)} %get-tuple-element.34.diag, f32[128,256]{1,0:T(8,128)} %get-tuple-element.35.across, f32[128,256]{1,0:T(8,128)} %copy-done.7, s32[1,8192]{1,0:T(1,128)} %retained.1), custom_call_target="tpu_custom_call" | custom-call | tf_op jit(solution)/shard_map/pallas_call | solution.py:273
  121.9 19.8 %all_to_all.5 = f32[32,8,128]{2,1,0:T(8,128)} all-to-all(f32[32,8,128]{2,1,0:T(8,128)} %shard_map.42), channel_id=1, replica_groups=mesh['energy'=32,'chain'=16] {'energy'}, dimensions={0} | all-to-all | bytes 262144 | tf_op jit(solution)/shard_map/all_to_all | solution.py:293
  141.8 1.8 %shard_map.43 = f32[2,32,256]{2,1,0:T(8,128)} custom-call(f32[256,128]{1,0:T(8,128)} %bitcast.4), custom_call_target="tpu_custom_call" | custom-call | tf_op jit(solution)/shard_map/pallas_call | solution.py:281
  143.6 1.5 %copy.4 = f32[2,32,1,256]{3,2,1,0:T(1,128)} copy(f32[2,32,1,256]{3,1,0,2:T(8,128)} %bitcast.5) | data formatting | bytes 131072 | tf_op jit(solution)/shard_map/reshape | solution.py:286
Async XLA Ops:
  0.0 11.0 %collective-permute-start = (f32[1,2,128,128]{3,2,1,0:T(8,128)}, f32[1,2,128,128]{3,2,1,0:T(8,128)S(1)}, u32[]{:S(2)}, u32[]{:S(2)}) collective-permute-start(f32[1,2,128,128]{3,2,1,0:T(8,128)} %coupling.1), channel_id=1, source_target_pairs={{0,1},{1,2},{2,3},{3,4},{4,5},{5,6},{6,7},{7,8},{8,9},{9,10},{10,1... | collective-permute-start | bytes 393224 | tf_op jit(solution)/shard_map/ppermute | solution.py:245
  11.0 0.7 copy-start.6
  13.8 6.5 %collective-permute-start.2 = (f32[128,512]{1,0:T(8,128)}, f32[128,512]{1,0:T(8,128)S(1)}, u32[]{:S(2)}, u32[]{:S(2)}) collective-permute-start(f32[128,512]{1,0:T(8,128)} %get-tuple-element.25), channel_id=1, source_target_pairs={{1,0},{2,1},{3,2},{4,3},{5,4},{6,5},{7,6},{8,7},{9,8},{10,9},{11,1... | collective-permute-start | bytes 786440 | tf_op jit(solution)/shard_map/ppermute | solution.py:245
  15.1 6.5 %collective-permute-start.1 = (f32[128,512]{1,0:T(8,128)}, f32[128,512]{1,0:T(8,128)S(1)}, u32[]{:S(2)}, u32[]{:S(2)}) collective-permute-start(f32[128,512]{1,0:T(8,128)} %get-tuple-element.25), channel_id=1, source_target_pairs={{0,1},{1,2},{2,3},{3,4},{4,5},{5,6},{6,7},{7,8},{8,9},{9,10},{10,1... | collective-permute-start | bytes 786440 | tf_op jit(solution)/shard_map/ppermute | solution.py:245
  20.3 1.3 copy-start
  21.6 0.7 copy-start.3
  31.8 14.9 %collective-permute-start.4 = (f32[128,512]{1,0:T(8,128)}, f32[128,512]{1,0:T(8,128)S(1)}, u32[]{:S(2)}, u32[]{:S(2)}) collective-permute-start(f32[128,512]{1,0:T(8,128)} %get-tuple-element.29), channel_id=1, source_target_pairs={{2,0},{3,1},{4,2},{5,3},{6,4},{7,5},{8,6},{9,7},{10,8},{11,9},{12,... | collective-permute-start | bytes 786440 | tf_op jit(solution)/shard_map/ppermute | solution.py:245
  33.0 14.9 %collective-permute-start.3 = (f32[128,512]{1,0:T(8,128)}, f32[128,512]{1,0:T(8,128)S(1)}, u32[]{:S(2)}, u32[]{:S(2)}) collective-permute-start(f32[128,512]{1,0:T(8,128)} %get-tuple-element.29), channel_id=1, source_target_pairs={{0,2},{1,3},{2,4},{3,5},{4,6},{5,7},{6,8},{7,9},{8,10},{9,11},{10,... | collective-permute-start | bytes 786440 | tf_op jit(solution)/shard_map/ppermute | solution.py:245
  46.7 1.3 copy-start.1
  48.0 0.7 copy-start.4
  58.1 18.8 %collective-permute-start.6 = (f32[128,512]{1,0:T(8,128)}, f32[128,512]{1,0:T(8,128)S(1)}, u32[]{:S(2)}, u32[]{:S(2)}) collective-permute-start(f32[128,512]{1,0:T(8,128)} %get-tuple-element.33), channel_id=1, source_target_pairs={{4,0},{5,1},{6,2},{7,3},{8,4},{9,5},{10,6},{11,7},{12,8},{13,9},{1... | collective-permute-start | bytes 786440 | tf_op jit(solution)/shard_map/ppermute | solution.py:245
  59.4 17.5 %collective-permute-start.5 = (f32[128,512]{1,0:T(8,128)}, f32[128,512]{1,0:T(8,128)S(1)}, u32[]{:S(2)}, u32[]{:S(2)}) collective-permute-start(f32[128,512]{1,0:T(8,128)} %get-tuple-element.33), channel_id=1, source_target_pairs={{0,4},{1,5},{2,6},{3,7},{4,8},{5,9},{6,10},{7,11},{8,12},{9,13},{1... | collective-permute-start | bytes 786440 | tf_op jit(solution)/shard_map/ppermute | solution.py:245
  76.9 0.7 copy-start.2
  76.9 0.8 copy-start.5
  87.1 17.2 %collective-permute-start.7 = (f32[128,256]{1,0:T(8,128)}, f32[128,256]{1,0:T(8,128)S(1)}, u32[]{:S(2)}, u32[]{:S(2)}) collective-permute-start(f32[128,256]{1,0:T(8,128)} %get-tuple-element.36), channel_id=1, source_target_pairs={{0,8},{1,9},{2,10},{3,11},{4,12},{5,13},{6,14},{7,15},{8,0},{9,1},... | collective-permute-start | bytes 393224 | tf_op jit(solution)/shard_map/ppermute | solution.py:272
  104.3 0.7 copy-start.7

commit v2 on v1

v2 whole, which is shorter than its diff:
```python
import jax
import jax.numpy as jnp
from jax import lax
from jax.experimental import pallas as pl
from jax.experimental.pallas import tpu as pltpu
from jax.sharding import PartitionSpec as P

ORB = 128
BROADENING = 0.04
PANEL = 32
UNROLL = 4
F32 = jnp.float32
CHAINS = 16


def product(left, right):
    return jnp.dot(left, right, precision=lax.Precision.HIGHEST, preferred_element_type=F32)


def rep(packed):
    real, imag = packed[:, :ORB], packed[:, ORB:]
    upper = jnp.concatenate([real, imag], axis=1)
    lower = jnp.concatenate([-imag, real], axis=1)
    return jnp.concatenate([upper, lower], axis=0)


def adjoint(packed):
    return jnp.concatenate([packed[:, :ORB].T, -packed[:, ORB:].T], axis=1)


def cmul(a, b):
    return a[0] * b[0] - a[1] * b[1], a[0] * b[1] + a[1] * b[0]


def cadd(a, b):
    return a[0] + b[0], a[1] + b[1]


def lanes(x, j):
    return jnp.broadcast_to(x[..., j : j + 1], x.shape)


def sublanes(tile, k):
    return jnp.take_along_axis(tile, jnp.full((8, 128), k, jnp.int32), axis=0)


def pivots(real, imag, own, others):
    lane = lax.broadcasted_iota(jnp.int32, (8, 128), 1)
    row = lax.broadcasted_iota(jnp.int32, (8, 128), 0)
    j = 8 * own
    cols = {
        u: [(lanes(real[u], j + c), lanes(imag[u], j + c)) for c in range(8)]
        for u in [own] + others
    }
    ahead = list(cols[own])
    whole = (real[own], imag[own])
    for a in range(8):
        pr, pi = sublanes(ahead[a][0], a), sublanes(ahead[a][1], a)
        scale = 1.0 / (pr * pr + pi * pi)
        is_row = row == a
        factor = (jnp.where(is_row, -1.0, ahead[a][0]), jnp.where(is_row, 0.0, ahead[a][1]))

        def eliminate(y, is_col):
            er, ei = sublanes(y[0], a), sublanes(y[1], a)
            br, bi = jnp.where(is_row, 0.0, y[0]), jnp.where(is_row, 0.0, y[1])
            if is_col is not None:
                er, ei = jnp.where(is_col, 1.0, er), jnp.where(is_col, 0.0, ei)
                br, bi = jnp.where(is_col, 0.0, br), jnp.where(is_col, 0.0, bi)
            scaled = cmul(factor, (er * pr + ei * pi, ei * pr - er * pi))
            return br - scaled[0] * scale, bi - scaled[1] * scale

        for c in range(a + 1, 8):
            ahead[c] = eliminate(ahead[c], None)
        whole = eliminate(whole, lane == j + a)
    real[own], imag[own] = whole
    rows = [(sublanes(whole[0], c), sublanes(whole[1], c)) for c in range(8)]
    inside = (lane >= j) & (lane < j + 8)
    for u in others:
        terms = [cmul(cols[u][c], rows[c]) for c in range(8)]
        while len(terms) > 1:
            terms = [cadd(terms[2 * q], terms[2 * q + 1]) for q in range(len(terms) // 2)]
        real[u] = jnp.where(inside, 0.0, real[u]) - terms[0][0]
        imag[u] = jnp.where(inside, 0.0, imag[u]) - terms[0][1]


def invert(matrix):
    count, extra = ORB // 8, 2
    panel = PANEL // 8
    lane = lax.broadcasted_iota(jnp.int32, (8, 128), 1)
    real = [matrix[8 * u : 8 * u + 8, :ORB] for u in range(count)]
    imag = [matrix[8 * u : 8 * u + 8, ORB:] for u in range(count)]
    for start in range(0, count, panel):
        own = list(range(start, start + panel))
        soon = list(range(start + panel, min(start + panel + extra, count)))
        rest = [u % count for u in range(start + panel, start + count)]
        rest = [u for u in rest if u not in soon]
        s = slice(8 * start, 8 * start + PANEL)
        col_real = {u: real[u][:, s] for u in rest}
        col_imag = {u: imag[u][:, s] for u in rest}
        for q, t in enumerate(own):
            pivots(real, imag, t, own[q + 1 :] + soon + own[:q])
        table = rep(
            jnp.concatenate(
                [
                    jnp.concatenate([real[u] for u in own], axis=0),
                    jnp.concatenate([imag[u] for u in own], axis=0),
                ],
                axis=1,
            )
        )
        inside = (lane >= 8 * start) & (lane < 8 * start + PANEL)
        cut = panel - extra if soon else len(rest)
        for chunk in (rest[:cut], rest[cut:]):
            if chunk:
                sides = [
                    jnp.concatenate([col_real[u] for u in chunk], axis=0),
                    jnp.concatenate([col_imag[u] for u in chunk], axis=0),
                ]
                delta = product(jnp.concatenate(sides, axis=1), table)
                for n, u in enumerate(chunk):
                    part = delta[8 * n : 8 * n + 8]
                    real[u] = jnp.where(inside, 0.0, real[u]) - part[:, :ORB]
                    imag[u] = jnp.where(inside, 0.0, imag[u]) - part[:, ORB:]
    return jnp.concatenate(
        [jnp.concatenate(real, axis=0), jnp.concatenate(imag, axis=0)], axis=1
    )


PACKED = jax.ShapeDtypeStruct((ORB, 2 * ORB), F32)
DOUBLE = jax.ShapeDtypeStruct((ORB, 4 * ORB), F32)
VM = pl.BlockSpec(memory_space=pltpu.VMEM)
SM = pl.BlockSpec(memory_space=pltpu.SMEM)
W = 2 * ORB


def packed(raw):
    return jnp.concatenate([raw[0, 0], raw[0, 1]], axis=1)


def first_kernel(scalars, onsite, coupling, diag_out, upper_out, even_out, odd_out):
    energy = scalars[0]
    row = lax.broadcasted_iota(jnp.int32, (ORB, ORB), 0)
    column = lax.broadcasted_iota(jnp.int32, (ORB, ORB), 1)
    eye = row == column
    raw_real, raw_imag = onsite[0, 0], onsite[0, 1]
    real = jnp.where(eye, energy, 0.0) - 0.5 * (raw_real + raw_real.T)
    imag = jnp.where(eye, BROADENING, 0.0) - 0.5 * (raw_imag - raw_imag.T)
    diag_out[...] = jnp.concatenate([real, imag], axis=1)
    upper_out[...] = packed(coupling)

    @pl.when(scalars[1] > 0.5)
    def contact():
        coupler = packed(coupling)
        square = product(coupler, rep(adjoint(coupler)))
        diag_out[:, :ORB] = real - 0.5 * square[:, ORB:]
        diag_out[:, ORB:] = imag + 0.5 * square[:, :ORB]
        upper_out[...] = jnp.zeros_like(coupler)

    inverse = invert(diag_out[...])
    upper = upper_out[...]
    table = rep(upper)
    onward = product(adjoint(upper), rep(inverse))
    up = jnp.concatenate([product(onward, table), onward], axis=1)
    down = jnp.concatenate([inverse, product(inverse, table)], axis=1)
    even = scalars[2] > 0.5

    @pl.when(even)
    def store_even():
        even_out[...] = up
        odd_out[...] = down

    @pl.when(jnp.logical_not(even))
    def store_odd():
        even_out[...] = down
        odd_out[...] = up


def second_kernel(
    scalars, diag, coupler, before, even_in, odd_in, diag_out, lower_out, upper_out, send_out
):
    even = scalars[2] > 0.5
    left = jnp.where(even, odd_in[...], even_in[...])
    right = jnp.where(even, even_in[...], odd_in[...])
    upper = coupler[...]
    from_right = product(product(upper, rep(right[:, :W])), rep(adjoint(upper)))
    new_diag = diag[...] - left[:, :W] - from_right
    diag_out[...] = new_diag
    new_lower = -product(left[:, W:], rep(adjoint(packed(before))))
    new_upper = -product(upper, rep(right[:, W:]))
    lower_out[...] = new_lower
    upper_out[...] = new_upper
    inverse = invert(new_diag)
    send_out[:, :W] = product(inverse, rep(new_upper))
    send_out[:, W:] = product(inverse, rep(new_lower))


def folded(diag, lower, upper, left, right):
    sides = jnp.concatenate([lower[...], upper[...]], axis=1)
    tables = jnp.concatenate([rep(left[:, :W]), rep(right[:, W:])], axis=0)
    return diag[...] - product(sides, tables)


def third_kernel(diag, lower, upper, left, right, diag_out, lower_out, upper_out, send_out):
    new_diag = folded(diag, lower, upper, left, right)
    diag_out[...] = new_diag
    new_lower = -product(lower[...], rep(left[:, W:]))
    new_upper = -product(upper[...], rep(right[:, :W]))
    lower_out[...] = new_lower
    upper_out[...] = new_upper
    inverse = invert(new_diag)
    send_out[:, :W] = product(inverse, rep(new_upper))
    send_out[:, W:] = product(inverse, rep(new_lower))


def fourth_kernel(diag, lower, upper, left, right, diag_out, across_out, send_out):
    new_diag = folded(diag, lower, upper, left, right)
    diag_out[...] = new_diag
    sides = jnp.concatenate([lower[...], upper[...]], axis=1)
    tables = jnp.concatenate([rep(left[:, W:]), rep(right[:, :W])], axis=0)
    across = -product(sides, tables)
    across_out[...] = across
    inverse = invert(new_diag)
    send_out[...] = product(inverse, rep(across))


def last_kernel(diag, across, partner, retained, out):
    green = invert(diag[...] - product(across[...], rep(partner[...])))
    real, imag = green[:, :ORB], green[:, ORB:]
    stack = jnp.concatenate([real.T, imag.T, real, imag], axis=0)
    high = stack.astype(jnp.bfloat16)
    middle = (stack - high.astype(F32)).astype(jnp.bfloat16)
    table = jnp.concatenate([high, middle], axis=1)
    rows = lax.broadcasted_iota(jnp.int32, (ORB, 256), 0)

    def chunk(step, carry):
        index = retained[0:1, pl.ds(pl.multiple_of(step * 256, 256), 256)]
        first = rows == (index >> 7)
        second = rows == (index & 127)
        hot = jnp.where(first, 1.0, 0.0).astype(jnp.bfloat16)
        picked = jnp.dot(
            table, jnp.concatenate([hot, hot], axis=0), preferred_element_type=F32
        )
        tile = []
        for part in range(4):
            chosen = jnp.where(second, picked[part * ORB : (part + 1) * ORB], 0.0)
            partial = jnp.sum(chosen.reshape(16, 8, 256), axis=0)
            for half in range(2):
                piece = partial[:, half * 128 : (half + 1) * 128]
                tile.append(jnp.sum(piece, axis=0, keepdims=True))
        out[step] = jnp.concatenate(tile, axis=0)
        return carry

    lax.fori_loop(0, 32, chunk, 0, unroll=UNROLL)


def correlate_kernel(received, out, second_real, second_imag):
    for half in range(2):
        s = slice(half * 128, (half + 1) * 128)
        ar = received[pl.ds(0 + half, 32, stride=8), :]
        ai = received[pl.ds(2 + half, 32, stride=8), :]
        br = received[pl.ds(4 + half, 32, stride=8), :]
        bi = received[pl.ds(6 + half, 32, stride=8), :]
        second_real[0:32, :] = br
        second_real[32:64, :] = br
        second_imag[0:32, :] = bi
        second_imag[32:64, :] = bi
        total_real = jnp.zeros((32, 128), F32)
        total_imag = jnp.zeros((32, 128), F32)
        for n in range(32):
            x = (
                jnp.broadcast_to(ar[n : n + 1, :], (32, 128)),
                jnp.broadcast_to(ai[n : n + 1, :], (32, 128)),
            )
            term = cmul(x, (second_real[n : n + 32, :], second_imag[n : n + 32, :]))
            total_real += term[0]
            total_imag += term[1]
        out[0, :, 0, s] = total_real
        out[1, :, 0, s] = total_imag


def green_pairs(onsite, coupling, retained, energy):
    position = lax.axis_index("chain")
    last = (position == CHAINS - 1).astype(F32)
    even = (position % 2 == 0).astype(F32)
    scalars = jnp.stack([energy, last, even])

    def moved(value, by):
        pairs = [(i, i + by) for i in range(CHAINS) if 0 <= i + by < CHAINS]
        return lax.ppermute(value, "chain", pairs)

    def swapped(value, start):
        pairs = [(i, i + 1) for i in range(start, CHAINS - 1, 2)]
        return lax.ppermute(value, "chain", pairs + [(b, a) for a, b in pairs])

    before = moved(coupling, 2)
    diag, upper, even_send, odd_send = pl.pallas_call(
        first_kernel,
        in_specs=[SM, VM, VM],
        out_shape=[PACKED, PACKED, DOUBLE, DOUBLE],
    )(scalars, onsite, coupling)
    before, even_send, odd_send = lax.optimization_barrier((before, even_send, odd_send))
    even_in = swapped(even_send, 0)
    odd_in = swapped(odd_send, 1)
    diag, lower, upper, send = pl.pallas_call(
        second_kernel,
        in_specs=[SM] + [VM] * 5,
        out_shape=[PACKED, PACKED, PACKED, DOUBLE],
    )(scalars, diag, upper, before, even_in, odd_in)
    left = moved(send, 2)
    right = moved(send, -2)
    diag, lower, upper, send = pl.pallas_call(
        third_kernel,
        out_shape=[PACKED, PACKED, PACKED, DOUBLE],
    )(diag, lower, upper, left, right)
    left = moved(send, 4)
    right = moved(send, -4)
    diag, across, send = pl.pallas_call(
        fourth_kernel,
        out_shape=[PACKED, PACKED, PACKED],
    )(diag, lower, upper, left, right)
    partner = lax.ppermute(send, "chain", [(i, (i + 8) % CHAINS) for i in range(CHAINS)])
    return pl.pallas_call(
        last_kernel,
        out_shape=jax.ShapeDtypeStruct((32, 8, 128), F32),
    )(diag, across, partner, retained)


def correlate(received):
    return pl.pallas_call(
        correlate_kernel,
        out_shape=jax.ShapeDtypeStruct((2, 32, 1, 256), F32),
        scratch_shapes=[pltpu.VMEM((64, 128), F32), pltpu.VMEM((64, 128), F32)],
    )(received.reshape(256, 128))


def shards(onsite, coupling, retained):
    groups = lax.axis_size("energy")
    energy = -2.0 + 4.0 * lax.axis_index("energy").astype(F32) / groups
    gathered = green_pairs(onsite, coupling, retained, energy)
    received = lax.all_to_all(gathered, "energy", split_axis=0, concat_axis=0, tiled=True)
    return correlate(received)


def solution(mesh):
    in_specs = (P("chain", None, None, None), P("chain", None, None, None), P("chain", None))
    out_specs = P(None, None, "chain", "energy")
    return jax.shard_map(shards, mesh=mesh, in_specs=in_specs, out_specs=out_specs, check_vma=False)
```

time: 146 us -> 129 us (0.88)
  Pallas kernels: 57.7 us -> 40.5 us
  local copies, waits for them, and re-layouts: 5.06 us -> 2.93 us
  waiting for transfers between devices: 21.6 us -> 23.2 us
    pallas_call x5 -> x4, Pallas kernels: 32.3 us -> 23.3 us  [the longest x1 7.16 us: green_pairs(): pl.pallas_call(second_kernel, in_specs=[SM] + [VM] * 5, out_shape=[PACKED...]
    pallas_call x1, Pallas kernels: 17 us -> 10.2 us  [green_pairs(): pl.pallas_call(last_kernel, out_shape=jax.ShapeDtypeStruct((32, 8, 128),...]
    ppermute x0 -> x2, starting transfers between devices: none -> 2.59 us  [swapped(): return lax.ppermute(value, 'chain', pairs + [(b, a) for a, b in pairs])]
    reshape x1 -> x0, local copies, waits for them, and re-layouts: 1.54 us -> none  [correlate(): return result.reshape(2, 32, 1, 256)]
    pallas_call x1, Pallas kernels: 8.54 us -> 7.03 us  [green_pairs(): pl.pallas_call(first_kernel, in_specs=[SM, VM, VM], out_shape=[PACKED, PA...]
    ppermute x7 -> x5, starting transfers between devices: 26.5 us -> 25.5 us  [moved(): return lax.ppermute(value, 'chain', pairs)]
    ppermute x7 -> x5, waiting for transfers between devices: 18 us -> 17.5 us  [moved(): return lax.ppermute(value, 'chain', pairs)]
  transfers between devices with their start and end apart: 8 -> 8, of which waited for: 5 -> 5; matrix products, arithmetic and copies ran while one was open for 0% -> 1% of each run, Pallas kernels for 6% -> 5%
where the time goes in v2:
time: 129 us
  starting transfers between devices  41.4 us (32%)
  Pallas kernels  40.5 us (31%)
  waiting for transfers between devices  23.2 us (18%)
  blocking collectives  19.8 us (15%)
  local copies, waits for them, and re-layouts  2.93 us (2%)
    ppermute x5, starting transfers between devices, moved(): return lax.ppermute(value, 'chain', pairs)  25.5 us
    all_to_all x1, blocking collectives, shards(): lax.all_to_all(gathered, 'energy', split_axis=0, concat_axis=0, tiled=True)  19.8 us
    ppermute x5, waiting for transfers between devices, moved(): return lax.ppermute(value, 'chain', pairs)  17.5 us
    ppermute x1, starting transfers between devices, green_pairs(): lax.ppermute(send, 'chain', [(i, (i + 8) % CHAINS) for i in range(CHAINS)])  13.4 us
    pallas_call x1, Pallas kernels, green_pairs(): pl.pallas_call(last_kernel, out_shape=jax.ShapeDtypeStruct((32, 8, 128),...  10.2 us
    pallas_call x1, Pallas kernels, green_pairs(): pl.pallas_call(second_kernel, in_specs=[SM] + [VM] * 5, out_shape=[PACKED...  7.16 us
    pallas_call x1, Pallas kernels, green_pairs(): pl.pallas_call(third_kernel, out_shape=[PACKED, PACKED, PACKED, DOUBLE])  7.12 us
    pallas_call x1, Pallas kernels, green_pairs(): pl.pallas_call(fourth_kernel, out_shape=[PACKED, PACKED, PACKED])  7.09 us
  transfers between devices with their start and end apart: 8, of which 5 were waited for; matrix products, arithmetic and copies ran while one was open for 1% of the time, Pallas kernels for 5%

profile of v2, /device:TPU:8, one launch (start us, length us, event | category | flops | bytes accessed | tf_op | source)
XLA Modules:
  0.0 128.6 jit_solution(10856910791434486538)
XLA Ops:
  0.0 4.3 %collective-permute-start = (f32[1,2,128,128]{3,2,1,0:T(8,128)}, f32[1,2,128,128]{3,2,1,0:T(8,128)S(1)}, u32[]{:S(2)}, u32[]{:S(2)}) collective-permute-start(f32[1,2,128,128]{3,2,1,0:T(8,128)} %coupling.1), channel_id=1, source_target_pairs={{0,2},{1,3},{2,4},{3,5},{4,6},{5,7},{6,8},{7,9},{8,10},{9,11},{10,... | collective-permute-start | bytes 393224 | tf_op jit(solution)/shard_map/ppermute | solution.py:289
  4.3 0.7 pad_maximum_fusion.scalars
  5.0 7.0 %shard_map.37 = (f32[128,256]{1,0:T(8,128)}, f32[128,256]{1,0:T(8,128)}, f32[128,512]{1,0:T(8,128)}, f32[128,512]{1,0:T(8,128)}) custom-call(f32[3]{0:T(128)} %pad_maximum_fusion.scalars, f32[1,2,128,128]{3,2,1,0:T(8,128)} %onsite.1, f32[1,2,128,128]{3,2,1,0:T(8,128)} %coupling.1), custom_call_target="tpu_custom_call" | custom-call | tf_op jit(solution)/shard_map/pallas_call | solution.py:296
  12.0 0.0 collective-permute-done.before
  12.0 0.0 copy-start.6
  12.0 1.9 %collective-permute-start.1 = (f32[128,512]{1,0:T(8,128)}, f32[128,512]{1,0:T(8,128)S(1)}, u32[]{:S(2)}, u32[]{:S(2)}) collective-permute-start(f32[128,512]{1,0:T(8,128)} %get-tuple-element.28), channel_id=1, source_target_pairs={{0,1},{2,3},{4,5},{6,7},{8,9},{10,11},{12,13},{14,15},{1,0},{3,2},... | collective-permute-start | bytes 786440 | tf_op jit(solution)/shard_map/ppermute | solution.py:293
  13.9 0.7 collective-permute-start.2
  14.6 1.0 collective-permute-done.1.even_in
  15.6 0.0 copy-start
  15.6 0.0 collective-permute-done.2.odd_in
  15.6 0.0 copy-start.2
  15.6 0.0 copy-done.6
  15.6 0.7 copy-done
  16.3 0.1 copy-done.2
  16.4 7.2 %shard_map.38 = (f32[128,256]{1,0:T(8,128)}, f32[128,256]{1,0:T(8,128)}, f32[128,256]{1,0:T(8,128)}, f32[128,512]{1,0:T(8,128)}) custom-call(f32[3]{0:T(128)} %pad_maximum_fusion.scalars, f32[128,256]{1,0:T(8,128)} %get-tuple-element.23.diag, f32[128,256]{1,0:T(8,128)} %get-tuple-element.24.coupler, f32[1,2,128,128]{3,2,1,0:T(8,128)} %copy-done.6, ...), custom_call_target="tpu_custom_call" | custom-call | tf_op jit(solution)/shard_map/pallas_call | solution.py:304
  23.6 1.3 collective-permute-start.4
  24.9 11.2 %collective-permute-start.3 = (f32[128,512]{1,0:T(8,128)}, f32[128,512]{1,0:T(8,128)S(1)}, u32[]{:S(2)}, u32[]{:S(2)}) collective-permute-start(f32[128,512]{1,0:T(8,128)} %get-tuple-element.33), channel_id=1, source_target_pairs={{0,2},{1,3},{2,4},{3,5},{4,6},{5,7},{6,8},{7,9},{8,10},{9,11},{10,... | collective-permute-start | bytes 786440 | tf_op jit(solution)/shard_map/ppermute | solution.py:289
  36.1 5.2 %collective-permute-done.4.right = f32[128,512]{1,0:T(8,128)S(1)} collective-permute-done((f32[128,512]{1,0:T(8,128)}, f32[128,512]{1,0:T(8,128)S(1)}, u32[]{:S(2)}, u32[]{:S(2)}) %collective-permute-start.4) | collective-permute-done | bytes 262176 | tf_op jit(solution)/shard_map/ppermute | solution.py:289
  41.2 0.0 copy-start.1
  41.2 1.4 %collective-permute-done.3.left = f32[128,512]{1,0:T(8,128)S(1)} collective-permute-done((f32[128,512]{1,0:T(8,128)}, f32[128,512]{1,0:T(8,128)S(1)}, u32[]{:S(2)}, u32[]{:S(2)}) %collective-permute-start.3) | collective-permute-done | bytes 262176 | tf_op jit(solution)/shard_map/ppermute | solution.py:289
  42.7 0.0 copy-start.4
  42.7 0.0 copy-done.1
  42.7 0.7 copy-done.4
  43.4 7.1 %shard_map.39 = (f32[128,256]{1,0:T(8,128)}, f32[128,256]{1,0:T(8,128)}, f32[128,256]{1,0:T(8,128)}, f32[128,512]{1,0:T(8,128)}) custom-call(f32[128,256]{1,0:T(8,128)} %get-tuple-element.30.diag, f32[128,256]{1,0:T(8,128)} %get-tuple-element.31.lower, f32[128,256]{1,0:T(8,128)} %get-tuple-element.32.upper, f32[128,512]{1,0:T(8,128)} %copy-done.4, ...), custom_call_target="tpu_custom_call" | custom-call | tf_op jit(solution)/shard_map/pallas_call | solution.py:311
  50.5 1.3 collective-permute-start.6
  51.8 7.4 %collective-permute-start.5 = (f32[128,512]{1,0:T(8,128)}, f32[128,512]{1,0:T(8,128)S(1)}, u32[]{:S(2)}, u32[]{:S(2)}) collective-permute-start(f32[128,512]{1,0:T(8,128)} %get-tuple-element.37), channel_id=1, source_target_pairs={{0,4},{1,5},{2,6},{3,7},{4,8},{5,9},{6,10},{7,11},{8,12},{9,13},{1... | collective-permute-start | bytes 786440 | tf_op jit(solution)/shard_map/ppermute | solution.py:289
  59.2 10.9 %collective-permute-done.6.right = f32[128,512]{1,0:T(8,128)S(1)} collective-permute-done((f32[128,512]{1,0:T(8,128)}, f32[128,512]{1,0:T(8,128)S(1)}, u32[]{:S(2)}, u32[]{:S(2)}) %collective-permute-start.6) | collective-permute-done | bytes 262176 | tf_op jit(solution)/shard_map/ppermute | solution.py:289
  70.1 0.0 copy-start.3
  70.1 0.0 collective-permute-done.5.left
  70.1 0.0 copy-start.5
  70.1 0.7 copy-done.3
  70.8 0.1 copy-done.5
  70.9 7.1 %shard_map.40 = (f32[128,256]{1,0:T(8,128)}, f32[128,256]{1,0:T(8,128)}, f32[128,256]{1,0:T(8,128)}) custom-call(f32[128,256]{1,0:T(8,128)} %get-tuple-element.34.diag, f32[128,256]{1,0:T(8,128)} %get-tuple-element.35.lower, f32[128,256]{1,0:T(8,128)} %get-tuple-element.36.upper, f32[128,512]{1,0:T(8,128)} %copy-done.5, f32[128,512]{1,0:T(8,128)} %copy-done.3), custom_call_target="tpu_custom_call" | custom-call | tf_op jit(solution)/shard_map/pallas_call | solution.py:317
  78.0 13.4 %collective-permute-start.7 = (f32[128,256]{1,0:T(8,128)}, f32[128,256]{1,0:T(8,128)S(1)}, u32[]{:S(2)}, u32[]{:S(2)}) collective-permute-start(f32[128,256]{1,0:T(8,128)} %get-tuple-element.40), channel_id=1, source_target_pairs={{0,8},{1,9},{2,10},{3,11},{4,12},{5,13},{6,14},{7,15},{8,0},{9,1},... | collective-permute-start | bytes 393224 | tf_op jit(solution)/shard_map/ppermute | solution.py:321
  91.4 4.7 %collective-permute-done.7.partner = f32[128,256]{1,0:T(8,128)S(1)} collective-permute-done((f32[128,256]{1,0:T(8,128)}, f32[128,256]{1,0:T(8,128)S(1)}, u32[]{:S(2)}, u32[]{:S(2)}) %collective-permute-start.7) | collective-permute-done | bytes 131104 | tf_op jit(solution)/shard_map/ppermute | solution.py:321
  96.1 0.0 copy-start.7
  96.1 0.6 copy-done.7
  96.7 10.2 %shard_map.41 = f32[32,8,128]{2,1,0:T(8,128)} custom-call(f32[128,256]{1,0:T(8,128)} %get-tuple-element.38.diag, f32[128,256]{1,0:T(8,128)} %get-tuple-element.39.across, f32[128,256]{1,0:T(8,128)} %copy-done.7, s32[1,8192]{1,0:T(1,128)} %retained.1), custom_call_target="tpu_custom_call" | custom-call | tf_op jit(solution)/shard_map/pallas_call | solution.py:322
  106.9 19.8 %all_to_all.5 = f32[32,8,128]{2,1,0:T(8,128)} all-to-all(f32[32,8,128]{2,1,0:T(8,128)} %shard_map.41), channel_id=1, replica_groups=mesh['energy'=32,'chain'=16] {'energy'}, dimensions={0} | all-to-all | bytes 262144 | tf_op jit(solution)/shard_map/all_to_all | solution.py:340
  126.7 1.9 %shard_map.42 = f32[2,32,1,256]{3,2,1,0:T(1,128)} custom-call(f32[256,128]{1,0:T(8,128)} %bitcast.4), custom_call_target="tpu_custom_call" | custom-call | tf_op jit(solution)/shard_map/pallas_call | solution.py:329
Async XLA Ops:
  0.0 12.0 %collective-permute-start = (f32[1,2,128,128]{3,2,1,0:T(8,128)}, f32[1,2,128,128]{3,2,1,0:T(8,128)S(1)}, u32[]{:S(2)}, u32[]{:S(2)}) collective-permute-start(f32[1,2,128,128]{3,2,1,0:T(8,128)} %coupling.1), channel_id=1, source_target_pairs={{0,2},{1,3},{2,4},{3,5},{4,6},{5,7},{6,8},{7,9},{8,10},{9,11},{10,... | collective-permute-start | bytes 393224 | tf_op jit(solution)/shard_map/ppermute | solution.py:289
  12.0 3.6 %copy-start.6 = (f32[1,2,128,128]{3,2,1,0:T(8,128)}, f32[1,2,128,128]{3,2,1,0:T(8,128)S(1)}, u32[]{:S(2)}) copy-start(f32[1,2,128,128]{3,2,1,0:T(8,128)S(1)} %collective-permute-done.before) | copy-start | bytes 393220
  12.0 3.6 %collective-permute-start.1 = (f32[128,512]{1,0:T(8,128)}, f32[128,512]{1,0:T(8,128)S(1)}, u32[]{:S(2)}, u32[]{:S(2)}) collective-permute-start(f32[128,512]{1,0:T(8,128)} %get-tuple-element.28), channel_id=1, source_target_pairs={{0,1},{2,3},{4,5},{6,7},{8,9},{10,11},{12,13},{14,15},{1,0},{3,2},... | collective-permute-start | bytes 786440 | tf_op jit(solution)/shard_map/ppermute | solution.py:293
  13.9 1.7 %collective-permute-start.2 = (f32[128,512]{1,0:T(8,128)}, f32[128,512]{1,0:T(8,128)S(1)}, u32[]{:S(2)}, u32[]{:S(2)}) collective-permute-start(f32[128,512]{1,0:T(8,128)} %get-tuple-element.29), channel_id=1, source_target_pairs={{1,2},{3,4},{5,6},{7,8},{9,10},{11,12},{13,14},{2,1},{4,3},{6,5},{... | collective-permute-start | bytes 786440 | tf_op jit(solution)/shard_map/ppermute | solution.py:293
  15.6 0.7 copy-start
  15.6 0.8 copy-start.2
  23.6 17.7 %collective-permute-start.4 = (f32[128,512]{1,0:T(8,128)}, f32[128,512]{1,0:T(8,128)S(1)}, u32[]{:S(2)}, u32[]{:S(2)}) collective-permute-start(f32[128,512]{1,0:T(8,128)} %get-tuple-element.33), channel_id=1, source_target_pairs={{2,0},{3,1},{4,2},{5,3},{6,4},{7,5},{8,6},{9,7},{10,8},{11,9},{12,... | collective-permute-start | bytes 786440 | tf_op jit(solution)/shard_map/ppermute | solution.py:289
  24.9 17.8 %collective-permute-start.3 = (f32[128,512]{1,0:T(8,128)}, f32[128,512]{1,0:T(8,128)S(1)}, u32[]{:S(2)}, u32[]{:S(2)}) collective-permute-start(f32[128,512]{1,0:T(8,128)} %get-tuple-element.33), channel_id=1, source_target_pairs={{0,2},{1,3},{2,4},{3,5},{4,6},{5,7},{6,8},{7,9},{8,10},{9,11},{10,... | collective-permute-start | bytes 786440 | tf_op jit(solution)/shard_map/ppermute | solution.py:289
  41.2 1.4 %copy-start.1 = (f32[128,512]{1,0:T(8,128)}, f32[128,512]{1,0:T(8,128)S(1)}, u32[]{:S(2)}) copy-start(f32[128,512]{1,0:T(8,128)S(1)} %collective-permute-done.4.right) | copy-start | bytes 786436
  42.7 0.7 copy-start.4
  50.5 19.6 %collective-permute-start.6 = (f32[128,512]{1,0:T(8,128)}, f32[128,512]{1,0:T(8,128)S(1)}, u32[]{:S(2)}, u32[]{:S(2)}) collective-permute-start(f32[128,512]{1,0:T(8,128)} %get-tuple-element.37), channel_id=1, source_target_pairs={{4,0},{5,1},{6,2},{7,3},{8,4},{9,5},{10,6},{11,7},{12,8},{13,9},{1... | collective-permute-start | bytes 786440 | tf_op jit(solution)/shard_map/ppermute | solution.py:289
  51.8 18.3 %collective-permute-start.5 = (f32[128,512]{1,0:T(8,128)}, f32[128,512]{1,0:T(8,128)S(1)}, u32[]{:S(2)}, u32[]{:S(2)}) collective-permute-start(f32[128,512]{1,0:T(8,128)} %get-tuple-element.37), channel_id=1, source_target_pairs={{0,4},{1,5},{2,6},{3,7},{4,8},{5,9},{6,10},{7,11},{8,12},{9,13},{1... | collective-permute-start | bytes 786440 | tf_op jit(solution)/shard_map/ppermute | solution.py:289
  70.1 0.7 copy-start.3
  70.1 0.8 copy-start.5
  78.0 18.1 %collective-permute-start.7 = (f32[128,256]{1,0:T(8,128)}, f32[128,256]{1,0:T(8,128)S(1)}, u32[]{:S(2)}, u32[]{:S(2)}) collective-permute-start(f32[128,256]{1,0:T(8,128)} %get-tuple-element.40), channel_id=1, source_target_pairs={{0,8},{1,9},{2,10},{3,11},{4,12},{5,13},{6,14},{7,15},{8,0},{9,1},... | collective-permute-start | bytes 393224 | tf_op jit(solution)/shard_map/ppermute | solution.py:321
  96.1 0.6 copy-start.7

commit v3 on v2

--- a/solution.py
+++ b/solution.py
@@ -59,6 +59,7 @@
         scale = 1.0 / (pr * pr + pi * pi)
         is_row = row == a
         factor = (jnp.where(is_row, -1.0, ahead[a][0]), jnp.where(is_row, 0.0, ahead[a][1]))
+        factor = cmul(factor, (pr, -pi))
 
         def eliminate(y, is_col):
             er, ei = sublanes(y[0], a), sublanes(y[1], a)
@@ -66,7 +67,7 @@
             if is_col is not None:
                 er, ei = jnp.where(is_col, 1.0, er), jnp.where(is_col, 0.0, ei)
                 br, bi = jnp.where(is_col, 0.0, br), jnp.where(is_col, 0.0, bi)
-            scaled = cmul(factor, (er * pr + ei * pi, ei * pr - er * pi))
+            scaled = cmul(factor, (er, ei))
             return br - scaled[0] * scale, bi - scaled[1] * scale
 
         for c in range(a + 1, 8):
@@ -126,10 +127,9 @@
     )
 
 
-PACKED = jax.ShapeDtypeStruct((ORB, 2 * ORB), F32)
-DOUBLE = jax.ShapeDtypeStruct((ORB, 4 * ORB), F32)
+PACKED = pltpu.VMEM((ORB, 2 * ORB), F32)
+DOUBLE = pltpu.VMEM((ORB, 4 * ORB), F32)
 VM = pl.BlockSpec(memory_space=pltpu.VMEM)
-SM = pl.BlockSpec(memory_space=pltpu.SMEM)
 W = 2 * ORB
 
 
@@ -137,8 +137,9 @@
     return jnp.concatenate([raw[0, 0], raw[0, 1]], axis=1)
 
 
-def first_kernel(scalars, onsite, coupling, diag_out, upper_out, even_out, odd_out):
-    energy = scalars[0]
+def first_kernel(onsite, coupling, diag_out, upper_out, even_out, odd_out):
+    position = lax.axis_index("chain")
+    energy = -2.0 + 4.0 * lax.axis_index("energy").astype(F32) / lax.axis_size("energy")
     row = lax.broadcasted_iota(jnp.int32, (ORB, ORB), 0)
     column = lax.broadcasted_iota(jnp.int32, (ORB, ORB), 1)
     eye = row == column
@@ -148,7 +149,7 @@
     diag_out[...] = jnp.concatenate([real, imag], axis=1)
     upper_out[...] = packed(coupling)
 
-    @pl.when(scalars[1] > 0.5)
+    @pl.when(position == CHAINS - 1)
     def contact():
         coupler = packed(coupling)
         square = product(coupler, rep(adjoint(coupler)))
@@ -162,7 +163,7 @@
     onward = product(adjoint(upper), rep(inverse))
     up = jnp.concatenate([product(onward, table), onward], axis=1)
     down = jnp.concatenate([inverse, product(inverse, table)], axis=1)
-    even = scalars[2] > 0.5
+    even = position % 2 == 0
 
     @pl.when(even)
     def store_even():
@@ -176,9 +177,9 @@
 
 
 def second_kernel(
-    scalars, diag, coupler, before, even_in, odd_in, diag_out, lower_out, upper_out, send_out
+    diag, coupler, before, odd_in, even_in, diag_out, lower_out, upper_out, send_out
 ):
-    even = scalars[2] > 0.5
+    even = lax.axis_index("chain") % 2 == 0
     left = jnp.where(even, odd_in[...], even_in[...])
     right = jnp.where(even, even_in[...], odd_in[...])
     upper = coupler[...]
@@ -278,12 +279,11 @@
         out[1, :, 0, s] = total_imag
 
 
-def green_pairs(onsite, coupling, retained, energy):
-    position = lax.axis_index("chain")
-    last = (position == CHAINS - 1).astype(F32)
-    even = (position % 2 == 0).astype(F32)
-    scalars = jnp.stack([energy, last, even])
-
+def near(*arrays):
+    return [pltpu.with_memory_space_constraint(x, pltpu.VMEM) for x in arrays]
+
+
+def green_pairs(onsite, coupling, retained):
     def moved(value, by):
         pairs = [(i, i + by) for i in range(CHAINS) if 0 <= i + by < CHAINS]
         return lax.ppermute(value, "chain", pairs)
@@ -295,48 +295,55 @@
     before = moved(coupling, 2)
     diag, upper, even_send, odd_send = pl.pallas_call(
         first_kernel,
-        in_specs=[SM, VM, VM],
+        in_specs=[VM, VM],
+        out_specs=[VM] * 4,
         out_shape=[PACKED, PACKED, DOUBLE, DOUBLE],
-    )(scalars, onsite, coupling)
+    )(onsite, coupling)
     before, even_send, odd_send = lax.optimization_barrier((before, even_send, odd_send))
+    odd_in = swapped(odd_send, 1)
     even_in = swapped(even_send, 0)
-    odd_in = swapped(odd_send, 1)
     diag, lower, upper, send = pl.pallas_call(
         second_kernel,
-        in_specs=[SM] + [VM] * 5,
+        in_specs=[VM] * 5,
+        out_specs=[VM] * 4,
         out_shape=[PACKED, PACKED, PACKED, DOUBLE],
-    )(scalars, diag, upper, before, even_in, odd_in)
+    )(*near(diag, upper, before, odd_in, even_in))
     left = moved(send, 2)
     right = moved(send, -2)
     diag, lower, upper, send = pl.pallas_call(
         third_kernel,
+        in_specs=[VM] * 5,
+        out_specs=[VM] * 4,
         out_shape=[PACKED, PACKED, PACKED, DOUBLE],
-    )(diag, lower, upper, left, right)
+    )(*near(diag, lower, upper, left, right))
     left = moved(send, 4)
     right = moved(send, -4)
     diag, across, send = pl.pallas_call(
         fourth_kernel,
+        in_specs=[VM] * 5,
+        out_specs=[VM] * 3,
         out_shape=[PACKED, PACKED, PACKED],
-    )(diag, lower, upper, left, right)
+    )(*near(diag, lower, upper, left, right))
     partner = lax.ppermute(send, "chain", [(i, (i + 8) % CHAINS) for i in range(CHAINS)])
     return pl.pallas_call(
         last_kernel,
-        out_shape=jax.ShapeDtypeStruct((32, 8, 128), F32),
-    )(diag, across, partner, retained)
+        in_specs=[VM] * 4,
+        out_specs=VM,
+        out_shape=pltpu.VMEM((32, 8, 128), F32),
+    )(*near(diag, across, partner), retained)
 
 
 def correlate(received):
     return pl.pallas_call(
         correlate_kernel,
+        in_specs=[VM],
         out_shape=jax.ShapeDtypeStruct((2, 32, 1, 256), F32),
         scratch_shapes=[pltpu.VMEM((64, 128), F32), pltpu.VMEM((64, 128), F32)],
-    )(received.reshape(256, 128))
+    )(*near(received.reshape(256, 128)))
 
 
 def shards(onsite, coupling, retained):
-    groups = lax.axis_size("energy")
-    energy = -2.0 + 4.0 * lax.axis_index("energy").astype(F32) / groups
-    gathered = green_pairs(onsite, coupling, retained, energy)
+    gathered = green_pairs(onsite, coupling, retained)
     received = lax.all_to_all(gathered, "energy", split_axis=0, concat_axis=0, tiled=True)
     return correlate(received)
 

time: 129 us -> 112 us (0.87)
  Pallas kernels: 40.5 us -> 30.8 us
  local copies, waits for them, and re-layouts: 2.93 us -> 0 us
  starting transfers between devices: 41.4 us -> 39.4 us
    pallas_call x6, Pallas kernels: 40.5 us -> 30.8 us  [the longest x1 9.08 us: green_pairs(): pl.pallas_call(last_kernel, in_specs=[VM] * 4, out_specs=VM, out_shape=pl...]
    ppermute x5, starting transfers between devices: 25.5 us -> 20.2 us  [moved(): return lax.ppermute(value, 'chain', pairs)]
    ppermute x2, starting transfers between devices: 2.59 us -> 6.3 us  [swapped(): return lax.ppermute(value, 'chain', pairs + [(b, a) for a, b in pairs])]
    unnamed x16 -> x0, local copies, waits for them, and re-layouts: 2.93 us -> none
  transfers between devices with their start and end apart: 8 -> 8, of which waited for: 5 -> 5; matrix products, arithmetic and copies ran while one was open for 1% -> 0% of each run, Pallas kernels for 5% -> 5%
where the time goes in v3:
time: 112 us
  starting transfers between devices  39.4 us (35%)
  Pallas kernels  30.8 us (28%)
  waiting for transfers between devices  22 us (20%)
  blocking collectives  19.5 us (17%)
    ppermute x5, starting transfers between devices, moved(): return lax.ppermute(value, 'chain', pairs)  20.2 us
    all_to_all x1, blocking collectives, shards(): lax.all_to_all(gathered, 'energy', split_axis=0, concat_axis=0, tiled=True)  19.5 us
    ppermute x5, waiting for transfers between devices, moved(): return lax.ppermute(value, 'chain', pairs)  16.5 us
    ppermute x1, starting transfers between devices, green_pairs(): lax.ppermute(send, 'chain', [(i, (i + 8) % CHAINS) for i in range(CHAINS)])  12.9 us
    pallas_call x1, Pallas kernels, green_pairs(): pl.pallas_call(last_kernel, in_specs=[VM] * 4, out_specs=VM, out_shape=pl...  9.08 us
    ppermute x2, starting transfers between devices, swapped(): return lax.ppermute(value, 'chain', pairs + [(b, a) for a, b in pairs])  6.3 us
    pallas_call x1, Pallas kernels, green_pairs(): pl.pallas_call(first_kernel, in_specs=[VM, VM], out_specs=[VM] * 4, out_s...  5.86 us
    pallas_call x1, Pallas kernels, green_pairs(): pl.pallas_call(second_kernel, in_specs=[VM] * 5, out_specs=[VM] * 4, out_...  5 us
  transfers between devices with their start and end apart: 8, of which 5 were waited for; matrix products, arithmetic and copies ran while one was open for 0% of the time, Pallas kernels for 5%

profile of v3, /device:TPU:8, one launch (start us, length us, event | category | flops | bytes accessed | tf_op | source)
XLA Modules:
  0.0 111.9 jit_solution(3788869659005649834)
XLA Ops:
  0.0 4.3 %collective-permute-start = (f32[1,2,128,128]{3,2,1,0:T(8,128)}, f32[1,2,128,128]{3,2,1,0:T(8,128)S(1)}, u32[]{:S(2)}, u32[]{:S(2)}) collective-permute-start(f32[1,2,128,128]{3,2,1,0:T(8,128)} %coupling.1), channel_id=1, source_target_pairs={{0,2},{1,3},{2,4},{3,5},{4,6},{5,7},{6,8},{7,9},{8,10},{9,11},{10,... | collective-permute-start | bytes 393224 | tf_op jit(solution)/shard_map/ppermute | solution.py:289
  4.3 5.9 %shard_map.37 = (f32[128,256]{1,0:T(8,128)S(1)}, f32[128,256]{1,0:T(8,128)S(1)}, f32[128,512]{1,0:T(8,128)S(1)}, f32[128,512]{1,0:T(8,128)S(1)}) custom-call(f32[1,2,128,128]{3,2,1,0:T(8,128)} %onsite.1, f32[1,2,128,128]{3,2,1,0:T(8,128)} %coupling.1), custom_call_target="tpu_custom_call" | custom-call | tf_op jit(solution)/shard_map/pallas_call | solution.py:296
  10.1 0.0 collective-permute-done.before
  10.2 0.7 collective-permute-start.1
  10.8 5.6 %collective-permute-start.2 = (f32[128,512]{1,0:T(8,128)S(1)}, f32[128,512]{1,0:T(8,128)S(1)}, u32[]{:S(2)}, u32[]{:S(2)}) collective-permute-start(f32[128,512]{1,0:T(8,128)S(1)} %get-tuple-element.29), channel_id=1, source_target_pairs={{0,1},{2,3},{4,5},{6,7},{8,9},{10,11},{12,13},{14,15},{1,0},{3,2},... | collective-permute-start | bytes 786440 | tf_op jit(solution)/shard_map/ppermute | solution.py:293
  16.5 0.0 collective-permute-done.1.odd_in
  16.5 1.1 %collective-permute-done.2.even_in = f32[128,512]{1,0:T(8,128)S(1)} collective-permute-done((f32[128,512]{1,0:T(8,128)S(1)}, f32[128,512]{1,0:T(8,128)S(1)}, u32[]{:S(2)}, u32[]{:S(2)}) %collective-permute-start.2) | collective-permute-done | bytes 262176 | tf_op jit(solution)/shard_map/ppermute | solution.py:293
  17.6 5.0 %shard_map.38 = (f32[128,256]{1,0:T(8,128)S(1)}, f32[128,256]{1,0:T(8,128)S(1)}, f32[128,256]{1,0:T(8,128)S(1)}, f32[128,512]{1,0:T(8,128)S(1)}) custom-call(f32[128,256]{1,0:T(8,128)S(1)} %get-tuple-element.23.diag, f32[128,256]{1,0:T(8,128)S(1)} %get-tuple-element.24.coupler, f32[1,2,128,128]{3,2,1,0:T(8,128)S(1)} %collective-permute-done.before, ...), custom_call_target="tpu_custom_call" | custom-call | tf_op jit(solution)/shard_map/pallas_call | solution.py:305
  22.6 1.3 %collective-permute-start.4 = (f32[128,512]{1,0:T(8,128)S(1)}, f32[128,512]{1,0:T(8,128)S(1)}, u32[]{:S(2)}, u32[]{:S(2)}) collective-permute-start(f32[128,512]{1,0:T(8,128)S(1)} %get-tuple-element.33), channel_id=1, source_target_pairs={{2,0},{3,1},{4,2},{5,3},{6,4},{7,5},{8,6},{9,7},{10,8},{11,9},{12,... | collective-permute-start | bytes 786440 | tf_op jit(solution)/shard_map/ppermute | solution.py:289
  23.9 5.3 %collective-permute-start.3 = (f32[128,512]{1,0:T(8,128)S(1)}, f32[128,512]{1,0:T(8,128)S(1)}, u32[]{:S(2)}, u32[]{:S(2)}) collective-permute-start(f32[128,512]{1,0:T(8,128)S(1)} %get-tuple-element.33), channel_id=1, source_target_pairs={{0,2},{1,3},{2,4},{3,5},{4,6},{5,7},{6,8},{7,9},{8,10},{9,11},{10,... | collective-permute-start | bytes 786440 | tf_op jit(solution)/shard_map/ppermute | solution.py:289
  29.3 5.0 %collective-permute-done.4.right = f32[128,512]{1,0:T(8,128)S(1)} collective-permute-done((f32[128,512]{1,0:T(8,128)S(1)}, f32[128,512]{1,0:T(8,128)S(1)}, u32[]{:S(2)}, u32[]{:S(2)}) %collective-permute-start.4) | collective-permute-done | bytes 262176 | tf_op jit(solution)/shard_map/ppermute | solution.py:289
  34.2 1.3 %collective-permute-done.3.left = f32[128,512]{1,0:T(8,128)S(1)} collective-permute-done((f32[128,512]{1,0:T(8,128)S(1)}, f32[128,512]{1,0:T(8,128)S(1)}, u32[]{:S(2)}, u32[]{:S(2)}) %collective-permute-start.3) | collective-permute-done | bytes 262176 | tf_op jit(solution)/shard_map/ppermute | solution.py:289
  35.5 5.0 %shard_map.39 = (f32[128,256]{1,0:T(8,128)S(1)}, f32[128,256]{1,0:T(8,128)S(1)}, f32[128,256]{1,0:T(8,128)S(1)}, f32[128,512]{1,0:T(8,128)S(1)}) custom-call(f32[128,256]{1,0:T(8,128)S(1)} %get-tuple-element.30.diag, f32[128,256]{1,0:T(8,128)S(1)} %get-tuple-element.31.lower, f32[128,256]{1,0:T(8,128)S(1)} %get-tuple-element.32.upper, ...), custom_call_target="tpu_custom_call" | custom-call | tf_op jit(solution)/shard_map/pallas_call | solution.py:313
  40.5 1.3 %collective-permute-start.6 = (f32[128,512]{1,0:T(8,128)S(1)}, f32[128,512]{1,0:T(8,128)S(1)}, u32[]{:S(2)}, u32[]{:S(2)}) collective-permute-start(f32[128,512]{1,0:T(8,128)S(1)} %get-tuple-element.37), channel_id=1, source_target_pairs={{4,0},{5,1},{6,2},{7,3},{8,4},{9,5},{10,6},{11,7},{12,8},{13,9},{1... | collective-permute-start | bytes 786440 | tf_op jit(solution)/shard_map/ppermute | solution.py:289
  41.8 8.0 %collective-permute-start.5 = (f32[128,512]{1,0:T(8,128)S(1)}, f32[128,512]{1,0:T(8,128)S(1)}, u32[]{:S(2)}, u32[]{:S(2)}) collective-permute-start(f32[128,512]{1,0:T(8,128)S(1)} %get-tuple-element.37), channel_id=1, source_target_pairs={{0,4},{1,5},{2,6},{3,7},{4,8},{5,9},{6,10},{7,11},{8,12},{9,13},{1... | collective-permute-start | bytes 786440 | tf_op jit(solution)/shard_map/ppermute | solution.py:289
  49.8 10.2 %collective-permute-done.6.right = f32[128,512]{1,0:T(8,128)S(1)} collective-permute-done((f32[128,512]{1,0:T(8,128)S(1)}, f32[128,512]{1,0:T(8,128)S(1)}, u32[]{:S(2)}, u32[]{:S(2)}) %collective-permute-start.6) | collective-permute-done | bytes 262176 | tf_op jit(solution)/shard_map/ppermute | solution.py:289
  60.1 0.0 collective-permute-done.5.left
  60.1 5.0 %shard_map.40 = (f32[128,256]{1,0:T(8,128)S(1)}, f32[128,256]{1,0:T(8,128)S(1)}, f32[128,256]{1,0:T(8,128)S(1)}) custom-call(f32[128,256]{1,0:T(8,128)S(1)} %get-tuple-element.34.diag, f32[128,256]{1,0:T(8,128)S(1)} %get-tuple-element.35.lower, f32[128,256]{1,0:T(8,128)S(1)} %get-tuple-element.36.upper, f32[128,512]{1,0:T(8,128)S(1)} %collective-permute-done.5.left, ...), custom_call_target="tpu_custom_call" | custom-call | tf_op jit(solution)/shard_map/pallas_call | solution.py:321
  65.0 12.9 %collective-permute-start.7 = (f32[128,256]{1,0:T(8,128)S(1)}, f32[128,256]{1,0:T(8,128)S(1)}, u32[]{:S(2)}, u32[]{:S(2)}) collective-permute-start(f32[128,256]{1,0:T(8,128)S(1)} %get-tuple-element.40), channel_id=1, source_target_pairs={{0,8},{1,9},{2,10},{3,11},{4,12},{5,13},{6,14},{7,15},{8,0},{9,1},... | collective-permute-start | bytes 393224 | tf_op jit(solution)/shard_map/ppermute | solution.py:327
  78.0 4.3 %collective-permute-done.7.partner = f32[128,256]{1,0:T(8,128)S(1)} collective-permute-done((f32[128,256]{1,0:T(8,128)S(1)}, f32[128,256]{1,0:T(8,128)S(1)}, u32[]{:S(2)}, u32[]{:S(2)}) %collective-permute-start.7) | collective-permute-done | bytes 131104 | tf_op jit(solution)/shard_map/ppermute | solution.py:327
  82.3 9.1 %shard_map.41 = f32[32,8,128]{2,1,0:T(8,128)S(1)} custom-call(f32[128,256]{1,0:T(8,128)S(1)} %get-tuple-element.38.diag, f32[128,256]{1,0:T(8,128)S(1)} %get-tuple-element.39.across, f32[128,256]{1,0:T(8,128)S(1)} %collective-permute-done.7.partner, s32[1,8192]{1,0:T(1,128)} %retained.1), custom_call_target="tpu_custom_call" | custom-call | tf_op jit(solution)/shard_map/pallas_call | solution.py:328
  91.4 19.5 %all_to_all.5 = f32[32,8,128]{2,1,0:T(8,128)S(1)} all-to-all(f32[32,8,128]{2,1,0:T(8,128)S(1)} %shard_map.41), channel_id=1, replica_groups=mesh['energy'=32,'chain'=16] {'energy'}, dimensions={0} | all-to-all | bytes 262144 | tf_op jit(solution)/shard_map/all_to_all | solution.py:347
  110.9 1.0 shard_map.42
Async XLA Ops:
  0.0 10.1 %collective-permute-start = (f32[1,2,128,128]{3,2,1,0:T(8,128)}, f32[1,2,128,128]{3,2,1,0:T(8,128)S(1)}, u32[]{:S(2)}, u32[]{:S(2)}) collective-permute-start(f32[1,2,128,128]{3,2,1,0:T(8,128)} %coupling.1), channel_id=1, source_target_pairs={{0,2},{1,3},{2,4},{3,5},{4,6},{5,7},{6,8},{7,9},{8,10},{9,11},{10,... | collective-permute-start | bytes 393224 | tf_op jit(solution)/shard_map/ppermute | solution.py:289
  10.2 6.3 %collective-permute-start.1 = (f32[128,512]{1,0:T(8,128)S(1)}, f32[128,512]{1,0:T(8,128)S(1)}, u32[]{:S(2)}, u32[]{:S(2)}) collective-permute-start(f32[128,512]{1,0:T(8,128)S(1)} %get-tuple-element.28), channel_id=1, source_target_pairs={{1,2},{3,4},{5,6},{7,8},{9,10},{11,12},{13,14},{2,1},{4,3},{6,5},{... | collective-permute-start | bytes 786440 | tf_op jit(solution)/shard_map/ppermute | solution.py:293
  10.8 6.8 %collective-permute-start.2 = (f32[128,512]{1,0:T(8,128)S(1)}, f32[128,512]{1,0:T(8,128)S(1)}, u32[]{:S(2)}, u32[]{:S(2)}) collective-permute-start(f32[128,512]{1,0:T(8,128)S(1)} %get-tuple-element.29), channel_id=1, source_target_pairs={{0,1},{2,3},{4,5},{6,7},{8,9},{10,11},{12,13},{14,15},{1,0},{3,2},... | collective-permute-start | bytes 786440 | tf_op jit(solution)/shard_map/ppermute | solution.py:293
  22.6 11.6 %collective-permute-start.4 = (f32[128,512]{1,0:T(8,128)S(1)}, f32[128,512]{1,0:T(8,128)S(1)}, u32[]{:S(2)}, u32[]{:S(2)}) collective-permute-start(f32[128,512]{1,0:T(8,128)S(1)} %get-tuple-element.33), channel_id=1, source_target_pairs={{2,0},{3,1},{4,2},{5,3},{6,4},{7,5},{8,6},{9,7},{10,8},{11,9},{12,... | collective-permute-start | bytes 786440 | tf_op jit(solution)/shard_map/ppermute | solution.py:289
  23.9 11.6 %collective-permute-start.3 = (f32[128,512]{1,0:T(8,128)S(1)}, f32[128,512]{1,0:T(8,128)S(1)}, u32[]{:S(2)}, u32[]{:S(2)}) collective-permute-start(f32[128,512]{1,0:T(8,128)S(1)} %get-tuple-element.33), channel_id=1, source_target_pairs={{0,2},{1,3},{2,4},{3,5},{4,6},{5,7},{6,8},{7,9},{8,10},{9,11},{10,... | collective-permute-start | bytes 786440 | tf_op jit(solution)/shard_map/ppermute | solution.py:289
  40.5 19.6 %collective-permute-start.6 = (f32[128,512]{1,0:T(8,128)S(1)}, f32[128,512]{1,0:T(8,128)S(1)}, u32[]{:S(2)}, u32[]{:S(2)}) collective-permute-start(f32[128,512]{1,0:T(8,128)S(1)} %get-tuple-element.37), channel_id=1, source_target_pairs={{4,0},{5,1},{6,2},{7,3},{8,4},{9,5},{10,6},{11,7},{12,8},{13,9},{1... | collective-permute-start | bytes 786440 | tf_op jit(solution)/shard_map/ppermute | solution.py:289
  41.8 18.3 %collective-permute-start.5 = (f32[128,512]{1,0:T(8,128)S(1)}, f32[128,512]{1,0:T(8,128)S(1)}, u32[]{:S(2)}, u32[]{:S(2)}) collective-permute-start(f32[128,512]{1,0:T(8,128)S(1)} %get-tuple-element.37), channel_id=1, source_target_pairs={{0,4},{1,5},{2,6},{3,7},{4,8},{5,9},{6,10},{7,11},{8,12},{9,13},{1... | collective-permute-start | bytes 786440 | tf_op jit(solution)/shard_map/ppermute | solution.py:289
  65.0 17.3 %collective-permute-start.7 = (f32[128,256]{1,0:T(8,128)S(1)}, f32[128,256]{1,0:T(8,128)S(1)}, u32[]{:S(2)}, u32[]{:S(2)}) collective-permute-start(f32[128,256]{1,0:T(8,128)S(1)} %get-tuple-element.40), channel_id=1, source_target_pairs={{0,8},{1,9},{2,10},{3,11},{4,12},{5,13},{6,14},{7,15},{8,0},{9,1},... | collective-permute-start | bytes 393224 | tf_op jit(solution)/shard_map/ppermute | solution.py:327

commit v4 on v3

--- a/solution.py
+++ b/solution.py
@@ -8,7 +8,7 @@
 ORB = 128
 BROADENING = 0.04
 PANEL = 32
-UNROLL = 4
+UNROLL = 16
 F32 = jnp.float32
 CHAINS = 16
 
@@ -195,37 +195,38 @@
     send_out[:, W:] = product(inverse, rep(new_lower))
 
 
-def folded(diag, lower, upper, left, right):
+def third_kernel(
+    diag, lower, upper, left, right, diag_out, lower_out, upper_out, upward_out, downward_out
+):
     sides = jnp.concatenate([lower[...], upper[...]], axis=1)
     tables = jnp.concatenate([rep(left[:, :W]), rep(right[:, W:])], axis=0)
-    return diag[...] - product(sides, tables)
-
-
-def third_kernel(diag, lower, upper, left, right, diag_out, lower_out, upper_out, send_out):
-    new_diag = folded(diag, lower, upper, left, right)
+    new_diag = diag[...] - product(sides, tables)
     diag_out[...] = new_diag
     new_lower = -product(lower[...], rep(left[:, W:]))
     new_upper = -product(upper[...], rep(right[:, :W]))
     lower_out[...] = new_lower
     upper_out[...] = new_upper
     inverse = invert(new_diag)
-    send_out[:, :W] = product(inverse, rep(new_upper))
-    send_out[:, W:] = product(inverse, rep(new_lower))
-
-
-def fourth_kernel(diag, lower, upper, left, right, diag_out, across_out, send_out):
-    new_diag = folded(diag, lower, upper, left, right)
+    upward_out[...] = product(inverse, rep(new_upper))
+    downward_out[...] = product(inverse, rep(new_lower))
+
+
+def fourth_kernel(diag, lower, upper, left, right, diag_out, side_out, send_out):
+    sides = jnp.concatenate([lower[...], upper[...]], axis=1)
+    tables = jnp.concatenate([rep(left[...]), rep(right[...])], axis=0)
+    new_diag = diag[...] - product(sides, tables)
     diag_out[...] = new_diag
-    sides = jnp.concatenate([lower[...], upper[...]], axis=1)
-    tables = jnp.concatenate([rep(left[:, W:]), rep(right[:, :W])], axis=0)
-    across = -product(sides, tables)
-    across_out[...] = across
-    inverse = invert(new_diag)
-    send_out[...] = product(inverse, rep(across))
-
-
-def last_kernel(diag, across, partner, retained, out):
-    green = invert(diag[...] - product(across[...], rep(partner[...])))
+    side = jnp.where(lax.axis_index("chain") < CHAINS // 2, upper[...], lower[...])
+    side_out[...] = side
+    send_out[...] = product(invert(new_diag), rep(side))
+
+
+def last_kernel(diag, side, left, right, left_late, right_late, partner, retained, out):
+    low = lax.axis_index("chain") < CHAINS // 2
+    outer = product(side[...], rep(left_late[...] + right_late[...]))
+    near_side = jnp.where(low, right[...], left[...])
+    inner = product(partner[...], rep(near_side))
+    green = invert(diag[...] - product(outer, rep(inner)))
     real, imag = green[:, :ORB], green[:, ORB:]
     stack = jnp.concatenate([real.T, imag.T, real, imag], axis=0)
     high = stack.astype(jnp.bfloat16)
@@ -310,27 +311,31 @@
     )(*near(diag, upper, before, odd_in, even_in))
     left = moved(send, 2)
     right = moved(send, -2)
-    diag, lower, upper, send = pl.pallas_call(
+    diag, lower, upper, upward, downward = pl.pallas_call(
         third_kernel,
         in_specs=[VM] * 5,
-        out_specs=[VM] * 4,
-        out_shape=[PACKED, PACKED, PACKED, DOUBLE],
+        out_specs=[VM] * 5,
+        out_shape=[PACKED] * 5,
     )(*near(diag, lower, upper, left, right))
-    left = moved(send, 4)
-    right = moved(send, -4)
-    diag, across, send = pl.pallas_call(
+    left = moved(upward, 4)
+    right = moved(downward, -4)
+    middle = range(CHAINS // 4, 3 * CHAINS // 4)
+    left_late = lax.ppermute(downward, "chain", [(i, i + 4) for i in middle])
+    right_late = lax.ppermute(upward, "chain", [(i, i - 4) for i in middle])
+    diag, side, send = pl.pallas_call(
         fourth_kernel,
         in_specs=[VM] * 5,
         out_specs=[VM] * 3,
-        out_shape=[PACKED, PACKED, PACKED],
+        out_shape=[PACKED] * 3,
     )(*near(diag, lower, upper, left, right))
+    send, left_late, right_late = lax.optimization_barrier((send, left_late, right_late))
     partner = lax.ppermute(send, "chain", [(i, (i + 8) % CHAINS) for i in range(CHAINS)])
     return pl.pallas_call(
         last_kernel,
-        in_specs=[VM] * 4,
+        in_specs=[VM] * 8,
         out_specs=VM,
         out_shape=pltpu.VMEM((32, 8, 128), F32),
-    )(*near(diag, across, partner), retained)
+    )(*near(diag, side, left, right, left_late, right_late, partner), retained)
 
 
 def correlate(received):

time: 112 us -> 111 us (level)
  the two profiles are of different devices: /device:TPU:8 before, /device:TPU:128 now
where the time goes in v4:
time: 111 us
  starting transfers between devices  38.4 us (35%)
  Pallas kernels  30.6 us (28%)
  waiting for transfers between devices  21.5 us (19%)
  blocking collectives  20.3 us (18%)
    ppermute x5, starting transfers between devices, moved(): return lax.ppermute(value, 'chain', pairs)  20.7 us
    all_to_all x1, blocking collectives, shards(): lax.all_to_all(gathered, 'energy', split_axis=0, concat_axis=0, tiled=True)  20.3 us
    ppermute x1, waiting for transfers between devices, green_pairs(): lax.ppermute(send, 'chain', [(i, (i + 8) % CHAINS) for i in range(CHAINS)])  10.6 us
    ppermute x5, waiting for transfers between devices, moved(): return lax.ppermute(value, 'chain', pairs)  9.78 us
    pallas_call x1, Pallas kernels, green_pairs(): pl.pallas_call(last_kernel, in_specs=[VM] * 8, out_specs=VM, out_shape=pl...  8.91 us
    ppermute x2, starting transfers between devices, swapped(): return lax.ppermute(value, 'chain', pairs + [(b, a) for a, b in pairs])  7.51 us
    ppermute x1, starting transfers between devices, green_pairs(): left_late = lax.ppermute(downward, 'chain', [(i, i + 4) for i in middle])  6.04 us
    pallas_call x1, Pallas kernels, green_pairs(): pl.pallas_call(first_kernel, in_specs=[VM, VM], out_specs=[VM] * 4, out_s...  5.86 us
  transfers between devices with their start and end apart: 10, of which 6 were waited for; matrix products, arithmetic and copies ran while one was open for 0% of the time, Pallas kernels for 10%

profile of v4, /device:TPU:128, one launch (start us, length us, event | category | flops | bytes accessed | tf_op | source)
XLA Modules:
  0.0 111.0 jit_solution(3854762989894214080)
XLA Ops:
  0.0 4.3 %collective-permute-start = (f32[1,2,128,128]{3,2,1,0:T(8,128)}, f32[1,2,128,128]{3,2,1,0:T(8,128)S(1)}, u32[]{:S(2)}, u32[]{:S(2)}) collective-permute-start(f32[1,2,128,128]{3,2,1,0:T(8,128)} %coupling.1), channel_id=1, source_target_pairs={{0,2},{1,3},{2,4},{3,5},{4,6},{5,7},{6,8},{7,9},{8,10},{9,11},{10,... | collective-permute-start | bytes 393224 | tf_op jit(solution)/shard_map/ppermute | solution.py:290
  4.3 5.9 %shard_map.37 = (f32[128,256]{1,0:T(8,128)S(1)}, f32[128,256]{1,0:T(8,128)S(1)}, f32[128,512]{1,0:T(8,128)S(1)}, f32[128,512]{1,0:T(8,128)S(1)}) custom-call(f32[1,2,128,128]{3,2,1,0:T(8,128)} %onsite.1, f32[1,2,128,128]{3,2,1,0:T(8,128)} %coupling.1), custom_call_target="tpu_custom_call" | custom-call | tf_op jit(solution)/shard_map/pallas_call | solution.py:297
  10.1 0.0 collective-permute-done.before
  10.2 1.9 %collective-permute-start.1 = (f32[128,512]{1,0:T(8,128)S(1)}, f32[128,512]{1,0:T(8,128)S(1)}, u32[]{:S(2)}, u32[]{:S(2)}) collective-permute-start(f32[128,512]{1,0:T(8,128)S(1)} %get-tuple-element.32), channel_id=1, source_target_pairs={{1,2},{3,4},{5,6},{7,8},{9,10},{11,12},{13,14},{2,1},{4,3},{6,5},{... | collective-permute-start | bytes 786440 | tf_op jit(solution)/shard_map/ppermute | solution.py:294
  12.1 5.6 %collective-permute-start.2 = (f32[128,512]{1,0:T(8,128)S(1)}, f32[128,512]{1,0:T(8,128)S(1)}, u32[]{:S(2)}, u32[]{:S(2)}) collective-permute-start(f32[128,512]{1,0:T(8,128)S(1)} %get-tuple-element.33), channel_id=1, source_target_pairs={{0,1},{2,3},{4,5},{6,7},{8,9},{10,11},{12,13},{14,15},{1,0},{3,2},... | collective-permute-start | bytes 786440 | tf_op jit(solution)/shard_map/ppermute | solution.py:294
  17.7 0.2 collective-permute-done.1.odd_in
  17.8 1.0 collective-permute-done.2.even_in
  18.8 5.0 %shard_map.38 = (f32[128,256]{1,0:T(8,128)S(1)}, f32[128,256]{1,0:T(8,128)S(1)}, f32[128,256]{1,0:T(8,128)S(1)}, f32[128,512]{1,0:T(8,128)S(1)}) custom-call(f32[128,256]{1,0:T(8,128)S(1)} %get-tuple-element.27.diag, f32[128,256]{1,0:T(8,128)S(1)} %get-tuple-element.28.coupler, f32[1,2,128,128]{3,2,1,0:T(8,128)S(1)} %collective-permute-done.before, ...), custom_call_target="tpu_custom_call" | custom-call | tf_op jit(solution)/shard_map/pallas_call | solution.py:306
  23.8 1.9 %collective-permute-start.4 = (f32[128,512]{1,0:T(8,128)S(1)}, f32[128,512]{1,0:T(8,128)S(1)}, u32[]{:S(2)}, u32[]{:S(2)}) collective-permute-start(f32[128,512]{1,0:T(8,128)S(1)} %get-tuple-element.37), channel_id=1, source_target_pairs={{2,0},{3,1},{4,2},{5,3},{6,4},{7,5},{8,6},{9,7},{10,8},{11,9},{12,... | collective-permute-start | bytes 786440 | tf_op jit(solution)/shard_map/ppermute | solution.py:290
  25.8 4.7 %collective-permute-start.3 = (f32[128,512]{1,0:T(8,128)S(1)}, f32[128,512]{1,0:T(8,128)S(1)}, u32[]{:S(2)}, u32[]{:S(2)}) collective-permute-start(f32[128,512]{1,0:T(8,128)S(1)} %get-tuple-element.37), channel_id=1, source_target_pairs={{0,2},{1,3},{2,4},{3,5},{4,6},{5,7},{6,8},{7,9},{8,10},{9,11},{10,... | collective-permute-start | bytes 786440 | tf_op jit(solution)/shard_map/ppermute | solution.py:290
  30.5 4.9 %collective-permute-done.4.right = f32[128,512]{1,0:T(8,128)S(1)} collective-permute-done((f32[128,512]{1,0:T(8,128)S(1)}, f32[128,512]{1,0:T(8,128)S(1)}, u32[]{:S(2)}, u32[]{:S(2)}) %collective-permute-start.4) | collective-permute-done | bytes 262176 | tf_op jit(solution)/shard_map/ppermute | solution.py:290
  35.4 1.4 %collective-permute-done.3.left = f32[128,512]{1,0:T(8,128)S(1)} collective-permute-done((f32[128,512]{1,0:T(8,128)S(1)}, f32[128,512]{1,0:T(8,128)S(1)}, u32[]{:S(2)}, u32[]{:S(2)}) %collective-permute-start.3) | collective-permute-done | bytes 262176 | tf_op jit(solution)/shard_map/ppermute | solution.py:290
  36.8 5.0 %shard_map.39 = (f32[128,256]{1,0:T(8,128)S(1)}, f32[128,256]{1,0:T(8,128)S(1)}, f32[128,256]{1,0:T(8,128)S(1)}, f32[128,256]{1,0:T(8,128)S(1)}, f32[128,256]{1,0:T(8,128)S(1)}) custom-call(f32[128,256]{1,0:T(8,128)S(1)} %get-tuple-element.34.diag, f32[128,256]{1,0:T(8,128)S(1)} %get-tuple-element.35.lower, f32[128,256]{1,0:T(8,128)S(1)} %get-tuple-element.36.upper, ...), custom_call_target="tpu_custom_call" | custom-call | tf_op jit(solution)/shard_map/pallas_call | solution.py:314
  41.8 7.9 %collective-permute-start.5 = (f32[128,256]{1,0:T(8,128)S(1)}, f32[128,256]{1,0:T(8,128)S(1)}, u32[]{:S(2)}, u32[]{:S(2)}) collective-permute-start(f32[128,256]{1,0:T(8,128)S(1)} %get-tuple-element.41), channel_id=1, source_target_pairs={{0,4},{1,5},{2,6},{3,7},{4,8},{5,9},{6,10},{7,11},{8,12},{9,13},{1... | collective-permute-start | bytes 393224 | tf_op jit(solution)/shard_map/ppermute | solution.py:290
  49.7 1.9 %collective-permute-start.6 = (f32[128,256]{1,0:T(8,128)S(1)}, f32[128,256]{1,0:T(8,128)S(1)}, u32[]{:S(2)}, u32[]{:S(2)}) collective-permute-start(f32[128,256]{1,0:T(8,128)S(1)} %get-tuple-element.42), channel_id=1, source_target_pairs={{4,0},{5,1},{6,2},{7,3},{8,4},{9,5},{10,6},{11,7},{12,8},{13,9},{1... | collective-permute-start | bytes 393224 | tf_op jit(solution)/shard_map/ppermute | solution.py:290
  51.7 1.9 %collective-permute-start.8 = (f32[128,256]{1,0:T(8,128)S(1)}, f32[128,256]{1,0:T(8,128)S(1)}, u32[]{:S(2)}, u32[]{:S(2)}) collective-permute-start(f32[128,256]{1,0:T(8,128)S(1)} %get-tuple-element.41), channel_id=1, source_target_pairs={{4,0},{5,1},{6,2},{7,3},{8,4},{9,5},{10,6},{11,7},{20,16},{21,17},... | collective-permute-start | bytes 393224 | tf_op jit(solution)/shard_map/ppermute | solution.py:324
  53.6 6.0 %collective-permute-start.7 = (f32[128,256]{1,0:T(8,128)S(1)}, f32[128,256]{1,0:T(8,128)S(1)}, u32[]{:S(2)}, u32[]{:S(2)}) collective-permute-start(f32[128,256]{1,0:T(8,128)S(1)} %get-tuple-element.42), channel_id=1, source_target_pairs={{4,8},{5,9},{6,10},{7,11},{8,12},{9,13},{10,14},{11,15},{20,24},{2... | collective-permute-start | bytes 393224 | tf_op jit(solution)/shard_map/ppermute | solution.py:323
  59.6 0.0 collective-permute-done.5.left
  59.6 3.4 %collective-permute-done.6.right = f32[128,256]{1,0:T(8,128)S(1)} collective-permute-done((f32[128,256]{1,0:T(8,128)S(1)}, f32[128,256]{1,0:T(8,128)S(1)}, u32[]{:S(2)}, u32[]{:S(2)}) %collective-permute-start.6) | collective-permute-done | bytes 131104 | tf_op jit(solution)/shard_map/ppermute | solution.py:290
  63.1 4.9 %shard_map.40 = (f32[128,256]{1,0:T(8,128)S(1)}, f32[128,256]{1,0:T(8,128)S(1)}, f32[128,256]{1,0:T(8,128)S(1)}) custom-call(f32[128,256]{1,0:T(8,128)S(1)} %get-tuple-element.38.diag, f32[128,256]{1,0:T(8,128)S(1)} %get-tuple-element.39.lower, f32[128,256]{1,0:T(8,128)S(1)} %get-tuple-element.40.upper, f32[128,256]{1,0:T(8,128)S(1)} %collective-permute-done.5.left, ...), custom_call_target="tpu_custom_call" | custom-call | tf_op jit(solution)/shard_map/pallas_call | solution.py:325
  68.0 0.0 collective-permute-done.8.right_late
  68.0 0.0 collective-permute-done.7.left_late
  68.0 2.1 %collective-permute-start.9 = (f32[128,256]{1,0:T(8,128)S(1)}, f32[128,256]{1,0:T(8,128)S(1)}, u32[]{:S(2)}, u32[]{:S(2)}) collective-permute-start(f32[128,256]{1,0:T(8,128)S(1)} %get-tuple-element.48), channel_id=1, source_target_pairs={{0,8},{1,9},{2,10},{3,11},{4,12},{5,13},{6,14},{7,15},{8,0},{9,1},... | collective-permute-start | bytes 393224 | tf_op jit(solution)/shard_map/ppermute | solution.py:332
  70.1 10.6 %collective-permute-done.9.partner = f32[128,256]{1,0:T(8,128)S(1)} collective-permute-done((f32[128,256]{1,0:T(8,128)S(1)}, f32[128,256]{1,0:T(8,128)S(1)}, u32[]{:S(2)}, u32[]{:S(2)}) %collective-permute-start.9) | collective-permute-done | bytes 131104 | tf_op jit(solution)/shard_map/ppermute | solution.py:332
  80.7 8.9 %shard_map.41 = f32[32,8,128]{2,1,0:T(8,128)S(1)} custom-call(f32[128,256]{1,0:T(8,128)S(1)} %get-tuple-element.43.diag, f32[128,256]{1,0:T(8,128)S(1)} %get-tuple-element.44.side, f32[128,256]{1,0:T(8,128)S(1)} %collective-permute-done.5.left, f32[128,256]{1,0:T(8,128)S(1)} %collective-permute-done.6.right, ...), custom_call_target="tpu_custom_call" | custom-call | tf_op jit(solution)/shard_map/pallas_call | solution.py:333
  89.7 20.3 %all_to_all.5 = f32[32,8,128]{2,1,0:T(8,128)S(1)} all-to-all(f32[32,8,128]{2,1,0:T(8,128)S(1)} %shard_map.41), channel_id=1, replica_groups=mesh['energy'=32,'chain'=16] {'energy'}, dimensions={0} | all-to-all | bytes 262144 | tf_op jit(solution)/shard_map/all_to_all | solution.py:352
  110.0 1.0 shard_map.42
Async XLA Ops:
  0.0 10.1 %collective-permute-start = (f32[1,2,128,128]{3,2,1,0:T(8,128)}, f32[1,2,128,128]{3,2,1,0:T(8,128)S(1)}, u32[]{:S(2)}, u32[]{:S(2)}) collective-permute-start(f32[1,2,128,128]{3,2,1,0:T(8,128)} %coupling.1), channel_id=1, source_target_pairs={{0,2},{1,3},{2,4},{3,5},{4,6},{5,7},{6,8},{7,9},{8,10},{9,11},{10,... | collective-permute-start | bytes 393224 | tf_op jit(solution)/shard_map/ppermute | solution.py:290
  10.2 7.7 %collective-permute-start.1 = (f32[128,512]{1,0:T(8,128)S(1)}, f32[128,512]{1,0:T(8,128)S(1)}, u32[]{:S(2)}, u32[]{:S(2)}) collective-permute-start(f32[128,512]{1,0:T(8,128)S(1)} %get-tuple-element.32), channel_id=1, source_target_pairs={{1,2},{3,4},{5,6},{7,8},{9,10},{11,12},{13,14},{2,1},{4,3},{6,5},{... | collective-permute-start | bytes 786440 | tf_op jit(solution)/shard_map/ppermute | solution.py:294
  12.1 6.7 %collective-permute-start.2 = (f32[128,512]{1,0:T(8,128)S(1)}, f32[128,512]{1,0:T(8,128)S(1)}, u32[]{:S(2)}, u32[]{:S(2)}) collective-permute-start(f32[128,512]{1,0:T(8,128)S(1)} %get-tuple-element.33), channel_id=1, source_target_pairs={{0,1},{2,3},{4,5},{6,7},{8,9},{10,11},{12,13},{14,15},{1,0},{3,2},... | collective-permute-start | bytes 786440 | tf_op jit(solution)/shard_map/ppermute | solution.py:294
  23.8 11.6 %collective-permute-start.4 = (f32[128,512]{1,0:T(8,128)S(1)}, f32[128,512]{1,0:T(8,128)S(1)}, u32[]{:S(2)}, u32[]{:S(2)}) collective-permute-start(f32[128,512]{1,0:T(8,128)S(1)} %get-tuple-element.37), channel_id=1, source_target_pairs={{2,0},{3,1},{4,2},{5,3},{6,4},{7,5},{8,6},{9,7},{10,8},{11,9},{12,... | collective-permute-start | bytes 786440 | tf_op jit(solution)/shard_map/ppermute | solution.py:290
  25.8 11.1 %collective-permute-start.3 = (f32[128,512]{1,0:T(8,128)S(1)}, f32[128,512]{1,0:T(8,128)S(1)}, u32[]{:S(2)}, u32[]{:S(2)}) collective-permute-start(f32[128,512]{1,0:T(8,128)S(1)} %get-tuple-element.37), channel_id=1, source_target_pairs={{0,2},{1,3},{2,4},{3,5},{4,6},{5,7},{6,8},{7,9},{8,10},{9,11},{10,... | collective-permute-start | bytes 786440 | tf_op jit(solution)/shard_map/ppermute | solution.py:290
  41.8 17.9 %collective-permute-start.5 = (f32[128,256]{1,0:T(8,128)S(1)}, f32[128,256]{1,0:T(8,128)S(1)}, u32[]{:S(2)}, u32[]{:S(2)}) collective-permute-start(f32[128,256]{1,0:T(8,128)S(1)} %get-tuple-element.41), channel_id=1, source_target_pairs={{0,4},{1,5},{2,6},{3,7},{4,8},{5,9},{6,10},{7,11},{8,12},{9,13},{1... | collective-permute-start | bytes 393224 | tf_op jit(solution)/shard_map/ppermute | solution.py:290
  49.7 13.3 %collective-permute-start.6 = (f32[128,256]{1,0:T(8,128)S(1)}, f32[128,256]{1,0:T(8,128)S(1)}, u32[]{:S(2)}, u32[]{:S(2)}) collective-permute-start(f32[128,256]{1,0:T(8,128)S(1)} %get-tuple-element.42), channel_id=1, source_target_pairs={{4,0},{5,1},{6,2},{7,3},{8,4},{9,5},{10,6},{11,7},{12,8},{13,9},{1... | collective-permute-start | bytes 393224 | tf_op jit(solution)/shard_map/ppermute | solution.py:290
  51.7 16.3 %collective-permute-start.8 = (f32[128,256]{1,0:T(8,128)S(1)}, f32[128,256]{1,0:T(8,128)S(1)}, u32[]{:S(2)}, u32[]{:S(2)}) collective-permute-start(f32[128,256]{1,0:T(8,128)S(1)} %get-tuple-element.41), channel_id=1, source_target_pairs={{4,0},{5,1},{6,2},{7,3},{8,4},{9,5},{10,6},{11,7},{20,16},{21,17},... | collective-permute-start | bytes 393224 | tf_op jit(solution)/shard_map/ppermute | solution.py:324
  53.6 14.4 %collective-permute-start.7 = (f32[128,256]{1,0:T(8,128)S(1)}, f32[128,256]{1,0:T(8,128)S(1)}, u32[]{:S(2)}, u32[]{:S(2)}) collective-permute-start(f32[128,256]{1,0:T(8,128)S(1)} %get-tuple-element.42), channel_id=1, source_target_pairs={{4,8},{5,9},{6,10},{7,11},{8,12},{9,13},{10,14},{11,15},{20,24},{2... | collective-permute-start | bytes 393224 | tf_op jit(solution)/shard_map/ppermute | solution.py:323
  68.0 12.8 %collective-permute-start.9 = (f32[128,256]{1,0:T(8,128)S(1)}, f32[128,256]{1,0:T(8,128)S(1)}, u32[]{:S(2)}, u32[]{:S(2)}) collective-permute-start(f32[128,256]{1,0:T(8,128)S(1)} %get-tuple-element.48), channel_id=1, source_target_pairs={{0,8},{1,9},{2,10},{3,11},{4,12},{5,13},{6,14},{7,15},{8,0},{9,1},... | collective-permute-start | bytes 393224 | tf_op jit(solution)/shard_map/ppermute | solution.py:332

commit v5 on v4

--- a/solution.py
+++ b/solution.py
@@ -335,7 +335,7 @@
         in_specs=[VM] * 8,
         out_specs=VM,
         out_shape=pltpu.VMEM((32, 8, 128), F32),
-    )(*near(diag, side, left, right, left_late, right_late, partner), retained)
+    )(*near(diag, side, left, right, left_late, right_late, partner, retained))
 
 
 def correlate(received):

time: 111 us -> 111 us (level)
  no operation moved by 1% of the time
where the time goes in v5:
time: 111 us; the launch traced here: 110 us
  starting transfers between devices  38.4 us (35%)
  Pallas kernels  29.8 us (27%)
  waiting for transfers between devices  21.5 us (19%)
  blocking collectives  20.3 us (18%)
    ppermute x5, starting transfers between devices, moved(): return lax.ppermute(value, 'chain', pairs)  20.7 us
    all_to_all x1, blocking collectives, shards(): lax.all_to_all(gathered, 'energy', split_axis=0, concat_axis=0, tiled=True)  20.3 us
    ppermute x1, waiting for transfers between devices, green_pairs(): lax.ppermute(send, 'chain', [(i, (i + 8) % CHAINS) for i in range(CHAINS)])  10.6 us
    ppermute x5, waiting for transfers between devices, moved(): return lax.ppermute(value, 'chain', pairs)  9.78 us
    pallas_call x1, Pallas kernels, green_pairs(): pl.pallas_call(last_kernel, in_specs=[VM] * 8, out_specs=VM, out_shape=pl...  8.13 us
    ppermute x2, starting transfers between devices, swapped(): return lax.ppermute(value, 'chain', pairs + [(b, a) for a, b in pairs])  7.51 us
    ppermute x1, starting transfers between devices, green_pairs(): left_late = lax.ppermute(downward, 'chain', [(i, i + 4) for i in middle])  6.04 us
    pallas_call x1, Pallas kernels, green_pairs(): pl.pallas_call(first_kernel, in_specs=[VM, VM], out_specs=[VM] * 4, out_s...  5.86 us
  transfers between devices with their start and end apart: 10, of which 6 were waited for; matrix products, arithmetic and copies ran while one was open for 0% of the time, Pallas kernels for 10%

profile of v5, /device:TPU:128, one launch (start us, length us, event | category | flops | bytes accessed | tf_op | source)
XLA Modules:
  0.0 110.2 jit_solution(3359422262389201834)
XLA Ops:
  0.0 4.3 %collective-permute-start = (f32[1,2,128,128]{3,2,1,0:T(8,128)}, f32[1,2,128,128]{3,2,1,0:T(8,128)S(1)}, u32[]{:S(2)}, u32[]{:S(2)}) collective-permute-start(f32[1,2,128,128]{3,2,1,0:T(8,128)} %coupling.1), channel_id=1, source_target_pairs={{0,2},{1,3},{2,4},{3,5},{4,6},{5,7},{6,8},{7,9},{8,10},{9,11},{10,... | collective-permute-start | bytes 393224 | tf_op jit(solution)/shard_map/ppermute | solution.py:290
  4.3 5.9 %shard_map.37 = (f32[128,256]{1,0:T(8,128)S(1)}, f32[128,256]{1,0:T(8,128)S(1)}, f32[128,512]{1,0:T(8,128)S(1)}, f32[128,512]{1,0:T(8,128)S(1)}) custom-call(f32[1,2,128,128]{3,2,1,0:T(8,128)} %onsite.1, f32[1,2,128,128]{3,2,1,0:T(8,128)} %coupling.1), custom_call_target="tpu_custom_call" | custom-call | tf_op jit(solution)/shard_map/pallas_call | solution.py:297
  10.1 0.0 collective-permute-done.before
  10.2 1.9 %collective-permute-start.1 = (f32[128,512]{1,0:T(8,128)S(1)}, f32[128,512]{1,0:T(8,128)S(1)}, u32[]{:S(2)}, u32[]{:S(2)}) collective-permute-start(f32[128,512]{1,0:T(8,128)S(1)} %get-tuple-element.32), channel_id=1, source_target_pairs={{1,2},{3,4},{5,6},{7,8},{9,10},{11,12},{13,14},{2,1},{4,3},{6,5},{... | collective-permute-start | bytes 786440 | tf_op jit(solution)/shard_map/ppermute | solution.py:294
  12.1 5.6 %collective-permute-start.2 = (f32[128,512]{1,0:T(8,128)S(1)}, f32[128,512]{1,0:T(8,128)S(1)}, u32[]{:S(2)}, u32[]{:S(2)}) collective-permute-start(f32[128,512]{1,0:T(8,128)S(1)} %get-tuple-element.33), channel_id=1, source_target_pairs={{0,1},{2,3},{4,5},{6,7},{8,9},{10,11},{12,13},{14,15},{1,0},{3,2},... | collective-permute-start | bytes 786440 | tf_op jit(solution)/shard_map/ppermute | solution.py:294
  17.7 0.2 collective-permute-done.1.odd_in
  17.8 1.0 collective-permute-done.2.even_in
  18.8 5.0 %shard_map.38 = (f32[128,256]{1,0:T(8,128)S(1)}, f32[128,256]{1,0:T(8,128)S(1)}, f32[128,256]{1,0:T(8,128)S(1)}, f32[128,512]{1,0:T(8,128)S(1)}) custom-call(f32[128,256]{1,0:T(8,128)S(1)} %get-tuple-element.27.diag, f32[128,256]{1,0:T(8,128)S(1)} %get-tuple-element.28.coupler, f32[1,2,128,128]{3,2,1,0:T(8,128)S(1)} %collective-permute-done.before, ...), custom_call_target="tpu_custom_call" | custom-call | tf_op jit(solution)/shard_map/pallas_call | solution.py:306
  23.8 1.9 %collective-permute-start.4 = (f32[128,512]{1,0:T(8,128)S(1)}, f32[128,512]{1,0:T(8,128)S(1)}, u32[]{:S(2)}, u32[]{:S(2)}) collective-permute-start(f32[128,512]{1,0:T(8,128)S(1)} %get-tuple-element.37), channel_id=1, source_target_pairs={{2,0},{3,1},{4,2},{5,3},{6,4},{7,5},{8,6},{9,7},{10,8},{11,9},{12,... | collective-permute-start | bytes 786440 | tf_op jit(solution)/shard_map/ppermute | solution.py:290
  25.8 4.7 %collective-permute-start.3 = (f32[128,512]{1,0:T(8,128)S(1)}, f32[128,512]{1,0:T(8,128)S(1)}, u32[]{:S(2)}, u32[]{:S(2)}) collective-permute-start(f32[128,512]{1,0:T(8,128)S(1)} %get-tuple-element.37), channel_id=1, source_target_pairs={{0,2},{1,3},{2,4},{3,5},{4,6},{5,7},{6,8},{7,9},{8,10},{9,11},{10,... | collective-permute-start | bytes 786440 | tf_op jit(solution)/shard_map/ppermute | solution.py:290
  30.5 4.9 %collective-permute-done.4.right = f32[128,512]{1,0:T(8,128)S(1)} collective-permute-done((f32[128,512]{1,0:T(8,128)S(1)}, f32[128,512]{1,0:T(8,128)S(1)}, u32[]{:S(2)}, u32[]{:S(2)}) %collective-permute-start.4) | collective-permute-done | bytes 262176 | tf_op jit(solution)/shard_map/ppermute | solution.py:290
  35.4 1.4 %collective-permute-done.3.left = f32[128,512]{1,0:T(8,128)S(1)} collective-permute-done((f32[128,512]{1,0:T(8,128)S(1)}, f32[128,512]{1,0:T(8,128)S(1)}, u32[]{:S(2)}, u32[]{:S(2)}) %collective-permute-start.3) | collective-permute-done | bytes 262176 | tf_op jit(solution)/shard_map/ppermute | solution.py:290
  36.8 5.0 %shard_map.39 = (f32[128,256]{1,0:T(8,128)S(1)}, f32[128,256]{1,0:T(8,128)S(1)}, f32[128,256]{1,0:T(8,128)S(1)}, f32[128,256]{1,0:T(8,128)S(1)}, f32[128,256]{1,0:T(8,128)S(1)}) custom-call(f32[128,256]{1,0:T(8,128)S(1)} %get-tuple-element.34.diag, f32[128,256]{1,0:T(8,128)S(1)} %get-tuple-element.35.lower, f32[128,256]{1,0:T(8,128)S(1)} %get-tuple-element.36.upper, ...), custom_call_target="tpu_custom_call" | custom-call | tf_op jit(solution)/shard_map/pallas_call | solution.py:314
  41.8 7.9 %collective-permute-start.5 = (f32[128,256]{1,0:T(8,128)S(1)}, f32[128,256]{1,0:T(8,128)S(1)}, u32[]{:S(2)}, u32[]{:S(2)}) collective-permute-start(f32[128,256]{1,0:T(8,128)S(1)} %get-tuple-element.41), channel_id=1, source_target_pairs={{0,4},{1,5},{2,6},{3,7},{4,8},{5,9},{6,10},{7,11},{8,12},{9,13},{1... | collective-permute-start | bytes 393224 | tf_op jit(solution)/shard_map/ppermute | solution.py:290
  49.7 1.9 %collective-permute-start.6 = (f32[128,256]{1,0:T(8,128)S(1)}, f32[128,256]{1,0:T(8,128)S(1)}, u32[]{:S(2)}, u32[]{:S(2)}) collective-permute-start(f32[128,256]{1,0:T(8,128)S(1)} %get-tuple-element.42), channel_id=1, source_target_pairs={{4,0},{5,1},{6,2},{7,3},{8,4},{9,5},{10,6},{11,7},{12,8},{13,9},{1... | collective-permute-start | bytes 393224 | tf_op jit(solution)/shard_map/ppermute | solution.py:290
  51.7 1.9 %collective-permute-start.8 = (f32[128,256]{1,0:T(8,128)S(1)}, f32[128,256]{1,0:T(8,128)S(1)}, u32[]{:S(2)}, u32[]{:S(2)}) collective-permute-start(f32[128,256]{1,0:T(8,128)S(1)} %get-tuple-element.41), channel_id=1, source_target_pairs={{4,0},{5,1},{6,2},{7,3},{8,4},{9,5},{10,6},{11,7},{20,16},{21,17},... | collective-permute-start | bytes 393224 | tf_op jit(solution)/shard_map/ppermute | solution.py:324
  53.6 6.0 %collective-permute-start.7 = (f32[128,256]{1,0:T(8,128)S(1)}, f32[128,256]{1,0:T(8,128)S(1)}, u32[]{:S(2)}, u32[]{:S(2)}) collective-permute-start(f32[128,256]{1,0:T(8,128)S(1)} %get-tuple-element.42), channel_id=1, source_target_pairs={{4,8},{5,9},{6,10},{7,11},{8,12},{9,13},{10,14},{11,15},{20,24},{2... | collective-permute-start | bytes 393224 | tf_op jit(solution)/shard_map/ppermute | solution.py:323
  59.6 0.0 collective-permute-done.5.left
  59.6 3.4 %collective-permute-done.6.right = f32[128,256]{1,0:T(8,128)S(1)} collective-permute-done((f32[128,256]{1,0:T(8,128)S(1)}, f32[128,256]{1,0:T(8,128)S(1)}, u32[]{:S(2)}, u32[]{:S(2)}) %collective-permute-start.6) | collective-permute-done | bytes 131104 | tf_op jit(solution)/shard_map/ppermute | solution.py:290
  63.1 0.0 copy-start
  63.1 4.9 %shard_map.40 = (f32[128,256]{1,0:T(8,128)S(1)}, f32[128,256]{1,0:T(8,128)S(1)}, f32[128,256]{1,0:T(8,128)S(1)}) custom-call(f32[128,256]{1,0:T(8,128)S(1)} %get-tuple-element.38.diag, f32[128,256]{1,0:T(8,128)S(1)} %get-tuple-element.39.lower, f32[128,256]{1,0:T(8,128)S(1)} %get-tuple-element.40.upper, f32[128,256]{1,0:T(8,128)S(1)} %collective-permute-done.5.left, ...), custom_call_target="tpu_custom_call" | custom-call | tf_op jit(solution)/shard_map/pallas_call | solution.py:325
  68.0 0.0 collective-permute-done.8.right_late
  68.0 0.0 collective-permute-done.7.left_late
  68.0 2.1 %collective-permute-start.9 = (f32[128,256]{1,0:T(8,128)S(1)}, f32[128,256]{1,0:T(8,128)S(1)}, u32[]{:S(2)}, u32[]{:S(2)}) collective-permute-start(f32[128,256]{1,0:T(8,128)S(1)} %get-tuple-element.48), channel_id=1, source_target_pairs={{0,8},{1,9},{2,10},{3,11},{4,12},{5,13},{6,14},{7,15},{8,0},{9,1},... | collective-permute-start | bytes 393224 | tf_op jit(solution)/shard_map/ppermute | solution.py:332
  70.1 10.6 %collective-permute-done.9.partner = f32[128,256]{1,0:T(8,128)S(1)} collective-permute-done((f32[128,256]{1,0:T(8,128)S(1)}, f32[128,256]{1,0:T(8,128)S(1)}, u32[]{:S(2)}, u32[]{:S(2)}) %collective-permute-start.9) | collective-permute-done | bytes 131104 | tf_op jit(solution)/shard_map/ppermute | solution.py:332
  80.7 0.0 copy-done
  80.7 8.1 %shard_map.41 = f32[32,8,128]{2,1,0:T(8,128)S(1)} custom-call(f32[128,256]{1,0:T(8,128)S(1)} %get-tuple-element.43.diag, f32[128,256]{1,0:T(8,128)S(1)} %get-tuple-element.44.side, f32[128,256]{1,0:T(8,128)S(1)} %collective-permute-done.5.left, f32[128,256]{1,0:T(8,128)S(1)} %collective-permute-done.6.right, ...), custom_call_target="tpu_custom_call" | custom-call | tf_op jit(solution)/shard_map/pallas_call | solution.py:333
  88.9 20.3 %all_to_all.5 = f32[32,8,128]{2,1,0:T(8,128)S(1)} all-to-all(f32[32,8,128]{2,1,0:T(8,128)S(1)} %shard_map.41), channel_id=1, replica_groups=mesh['energy'=32,'chain'=16] {'energy'}, dimensions={0} | all-to-all | bytes 262144 | tf_op jit(solution)/shard_map/all_to_all | solution.py:352
  109.2 1.0 shard_map.42
Async XLA Ops:
  0.0 10.1 %collective-permute-start = (f32[1,2,128,128]{3,2,1,0:T(8,128)}, f32[1,2,128,128]{3,2,1,0:T(8,128)S(1)}, u32[]{:S(2)}, u32[]{:S(2)}) collective-permute-start(f32[1,2,128,128]{3,2,1,0:T(8,128)} %coupling.1), channel_id=1, source_target_pairs={{0,2},{1,3},{2,4},{3,5},{4,6},{5,7},{6,8},{7,9},{8,10},{9,11},{10,... | collective-permute-start | bytes 393224 | tf_op jit(solution)/shard_map/ppermute | solution.py:290
  10.2 7.7 %collective-permute-start.1 = (f32[128,512]{1,0:T(8,128)S(1)}, f32[128,512]{1,0:T(8,128)S(1)}, u32[]{:S(2)}, u32[]{:S(2)}) collective-permute-start(f32[128,512]{1,0:T(8,128)S(1)} %get-tuple-element.32), channel_id=1, source_target_pairs={{1,2},{3,4},{5,6},{7,8},{9,10},{11,12},{13,14},{2,1},{4,3},{6,5},{... | collective-permute-start | bytes 786440 | tf_op jit(solution)/shard_map/ppermute | solution.py:294
  12.1 6.7 %collective-permute-start.2 = (f32[128,512]{1,0:T(8,128)S(1)}, f32[128,512]{1,0:T(8,128)S(1)}, u32[]{:S(2)}, u32[]{:S(2)}) collective-permute-start(f32[128,512]{1,0:T(8,128)S(1)} %get-tuple-element.33), channel_id=1, source_target_pairs={{0,1},{2,3},{4,5},{6,7},{8,9},{10,11},{12,13},{14,15},{1,0},{3,2},... | collective-permute-start | bytes 786440 | tf_op jit(solution)/shard_map/ppermute | solution.py:294
  23.8 11.6 %collective-permute-start.4 = (f32[128,512]{1,0:T(8,128)S(1)}, f32[128,512]{1,0:T(8,128)S(1)}, u32[]{:S(2)}, u32[]{:S(2)}) collective-permute-start(f32[128,512]{1,0:T(8,128)S(1)} %get-tuple-element.37), channel_id=1, source_target_pairs={{2,0},{3,1},{4,2},{5,3},{6,4},{7,5},{8,6},{9,7},{10,8},{11,9},{12,... | collective-permute-start | bytes 786440 | tf_op jit(solution)/shard_map/ppermute | solution.py:290
  25.8 11.1 %collective-permute-start.3 = (f32[128,512]{1,0:T(8,128)S(1)}, f32[128,512]{1,0:T(8,128)S(1)}, u32[]{:S(2)}, u32[]{:S(2)}) collective-permute-start(f32[128,512]{1,0:T(8,128)S(1)} %get-tuple-element.37), channel_id=1, source_target_pairs={{0,2},{1,3},{2,4},{3,5},{4,6},{5,7},{6,8},{7,9},{8,10},{9,11},{10,... | collective-permute-start | bytes 786440 | tf_op jit(solution)/shard_map/ppermute | solution.py:290
  41.8 17.9 %collective-permute-start.5 = (f32[128,256]{1,0:T(8,128)S(1)}, f32[128,256]{1,0:T(8,128)S(1)}, u32[]{:S(2)}, u32[]{:S(2)}) collective-permute-start(f32[128,256]{1,0:T(8,128)S(1)} %get-tuple-element.41), channel_id=1, source_target_pairs={{0,4},{1,5},{2,6},{3,7},{4,8},{5,9},{6,10},{7,11},{8,12},{9,13},{1... | collective-permute-start | bytes 393224 | tf_op jit(solution)/shard_map/ppermute | solution.py:290
  49.7 13.3 %collective-permute-start.6 = (f32[128,256]{1,0:T(8,128)S(1)}, f32[128,256]{1,0:T(8,128)S(1)}, u32[]{:S(2)}, u32[]{:S(2)}) collective-permute-start(f32[128,256]{1,0:T(8,128)S(1)} %get-tuple-element.42), channel_id=1, source_target_pairs={{4,0},{5,1},{6,2},{7,3},{8,4},{9,5},{10,6},{11,7},{12,8},{13,9},{1... | collective-permute-start | bytes 393224 | tf_op jit(solution)/shard_map/ppermute | solution.py:290
  51.7 16.3 %collective-permute-start.8 = (f32[128,256]{1,0:T(8,128)S(1)}, f32[128,256]{1,0:T(8,128)S(1)}, u32[]{:S(2)}, u32[]{:S(2)}) collective-permute-start(f32[128,256]{1,0:T(8,128)S(1)} %get-tuple-element.41), channel_id=1, source_target_pairs={{4,0},{5,1},{6,2},{7,3},{8,4},{9,5},{10,6},{11,7},{20,16},{21,17},... | collective-permute-start | bytes 393224 | tf_op jit(solution)/shard_map/ppermute | solution.py:324
  53.6 14.4 %collective-permute-start.7 = (f32[128,256]{1,0:T(8,128)S(1)}, f32[128,256]{1,0:T(8,128)S(1)}, u32[]{:S(2)}, u32[]{:S(2)}) collective-permute-start(f32[128,256]{1,0:T(8,128)S(1)} %get-tuple-element.42), channel_id=1, source_target_pairs={{4,8},{5,9},{6,10},{7,11},{8,12},{9,13},{10,14},{11,15},{20,24},{2... | collective-permute-start | bytes 393224 | tf_op jit(solution)/shard_map/ppermute | solution.py:323
  63.1 17.7 %copy-start = (s32[1,8192]{1,0:T(1,128)S(1)}, s32[1,8192]{1,0:T(1,128)}, u32[]{:S(2)}) copy-start(s32[1,8192]{1,0:T(1,128)} %retained.1) | copy-start | bytes 98308
  68.0 12.8 %collective-permute-start.9 = (f32[128,256]{1,0:T(8,128)S(1)}, f32[128,256]{1,0:T(8,128)S(1)}, u32[]{:S(2)}, u32[]{:S(2)}) collective-permute-start(f32[128,256]{1,0:T(8,128)S(1)} %get-tuple-element.48), channel_id=1, source_target_pairs={{0,8},{1,9},{2,10},{3,11},{4,12},{5,13},{6,14},{7,15},{8,0},{9,1},... | collective-permute-start | bytes 393224 | tf_op jit(solution)/shard_map/ppermute | solution.py:332

commit v6 on v5

--- a/solution.py
+++ b/solution.py
@@ -221,7 +221,7 @@
     send_out[...] = product(invert(new_diag), rep(side))
 
 
-def last_kernel(diag, side, left, right, left_late, right_late, partner, retained, out):
+def last_kernel(diag, side, left, right, left_late, right_late, partner, retained, hot, out):
     low = lax.axis_index("chain") < CHAINS // 2
     outer = product(side[...], rep(left_late[...] + right_late[...]))
     near_side = jnp.where(low, right[...], left[...])
@@ -235,12 +235,10 @@
     rows = lax.broadcasted_iota(jnp.int32, (ORB, 256), 0)
 
     def chunk(step, carry):
-        index = retained[0:1, pl.ds(pl.multiple_of(step * 256, 256), 256)]
-        first = rows == (index >> 7)
-        second = rows == (index & 127)
-        hot = jnp.where(first, 1.0, 0.0).astype(jnp.bfloat16)
+        s = pl.ds(pl.multiple_of(step * 256, 256), 256)
+        first, second = hot[:, s], rows == (retained[0:1, s] & 127)
         picked = jnp.dot(
-            table, jnp.concatenate([hot, hot], axis=0), preferred_element_type=F32
+            table, jnp.concatenate([first, first], axis=0), preferred_element_type=F32
         )
         tile = []
         for part in range(4):
@@ -253,6 +251,18 @@
         return carry
 
     lax.fori_loop(0, 32, chunk, 0, unroll=UNROLL)
+
+
+def hot_kernel(retained, hot):
+    rows = lax.broadcasted_iota(jnp.int32, (ORB, 256), 0)
+
+    def chunk(step, carry):
+        s = pl.ds(pl.multiple_of(step * 256, 256), 256)
+        index = retained[0:1, s]
+        hot[:, s] = jnp.where(rows == (index >> 7), 1.0, 0.0).astype(jnp.bfloat16)
+        return carry
+
+    lax.fori_loop(0, 32, chunk, 0, unroll=8)
 
 
 def correlate_kernel(received, out, second_real, second_imag):
@@ -328,14 +338,22 @@
         out_specs=[VM] * 3,
         out_shape=[PACKED] * 3,
     )(*near(diag, lower, upper, left, right))
-    send, left_late, right_late = lax.optimization_barrier((send, left_late, right_late))
+    send, left_late, right_late, listed = lax.optimization_barrier(
+        (send, left_late, right_late, retained)
+    )
     partner = lax.ppermute(send, "chain", [(i, (i + 8) % CHAINS) for i in range(CHAINS)])
+    hot = pl.pallas_call(
+        hot_kernel,
+        in_specs=[VM],
+        out_specs=VM,
+        out_shape=pltpu.VMEM((ORB, 8192), jnp.bfloat16),
+    )(listed)
     return pl.pallas_call(
         last_kernel,
-        in_specs=[VM] * 8,
+        in_specs=[VM] * 9,
         out_specs=VM,
         out_shape=pltpu.VMEM((32, 8, 128), F32),
-    )(*near(diag, side, left, right, left_late, right_late, partner, retained))
+    )(*near(diag, side, left, right, left_late, right_late, partner, retained, hot))
 
 
 def correlate(received):

time: 111 us -> 111 us (level)
  waiting for transfers between devices: 21.5 us -> 20 us
    ppermute x1, waiting for transfers between devices: 10.6 us -> 9.08 us  [green_pairs(): lax.ppermute(send, 'chain', [(i, (i + 8) % CHAINS) for i in range(CHAINS)])]
    pallas_call x1 -> x2, Pallas kernels: 8.13 us -> 9.24 us  [the longest x1 7.73 us: green_pairs(): pl.pallas_call(last_kernel, in_specs=[VM] * 9, out_specs=VM, out_shape=pl...]
  transfers between devices with their start and end apart: 10 -> 10, of which waited for: 6 -> 6; matrix products, arithmetic and copies ran while one was open for 0% -> 0% of each run, Pallas kernels for 10% -> 11%
where the time goes in v6:
time: 111 us
  starting transfers between devices  38.4 us (35%)
  Pallas kernels  30.9 us (28%)
  blocking collectives  20.3 us (18%)
  waiting for transfers between devices  20 us (18%)
    ppermute x5, starting transfers between devices, moved(): return lax.ppermute(value, 'chain', pairs)  20.8 us
    all_to_all x1, blocking collectives, shards(): lax.all_to_all(gathered, 'energy', split_axis=0, concat_axis=0, tiled=True)  20.3 us
    ppermute x5, waiting for transfers between devices, moved(): return lax.ppermute(value, 'chain', pairs)  9.78 us
    ppermute x1, waiting for transfers between devices, green_pairs(): lax.ppermute(send, 'chain', [(i, (i + 8) % CHAINS) for i in range(CHAINS)])  9.08 us
    pallas_call x1, Pallas kernels, green_pairs(): pl.pallas_call(last_kernel, in_specs=[VM] * 9, out_specs=VM, out_shape=pl...  7.73 us
    ppermute x2, starting transfers between devices, swapped(): return lax.ppermute(value, 'chain', pairs + [(b, a) for a, b in pairs])  7.51 us
    ppermute x1, starting transfers between devices, green_pairs(): left_late = lax.ppermute(downward, 'chain', [(i, i + 4) for i in middle])  6.04 us
    pallas_call x1, Pallas kernels, green_pairs(): pl.pallas_call(first_kernel, in_specs=[VM, VM], out_specs=[VM] * 4, out_s...  5.86 us
  transfers between devices with their start and end apart: 10, of which 6 were waited for; matrix products, arithmetic and copies ran while one was open for 0% of the time, Pallas kernels for 11%

profile of v6, /device:TPU:128, one launch (start us, length us, event | category | flops | bytes accessed | tf_op | source)
XLA Modules:
  0.0 110.7 jit_solution(11715347385059056662)
XLA Ops:
  0.0 4.3 %collective-permute-start = (f32[1,2,128,128]{3,2,1,0:T(8,128)}, f32[1,2,128,128]{3,2,1,0:T(8,128)S(1)}, u32[]{:S(2)}, u32[]{:S(2)}) collective-permute-start(f32[1,2,128,128]{3,2,1,0:T(8,128)} %coupling.1), channel_id=1, source_target_pairs={{0,2},{1,3},{2,4},{3,5},{4,6},{5,7},{6,8},{7,9},{8,10},{9,11},{10,... | collective-permute-start | bytes 393224 | tf_op jit(solution)/shard_map/ppermute | solution.py:300
  4.3 5.9 %shard_map.37 = (f32[128,256]{1,0:T(8,128)S(1)}, f32[128,256]{1,0:T(8,128)S(1)}, f32[128,512]{1,0:T(8,128)S(1)}, f32[128,512]{1,0:T(8,128)S(1)}) custom-call(f32[1,2,128,128]{3,2,1,0:T(8,128)} %onsite.1, f32[1,2,128,128]{3,2,1,0:T(8,128)} %coupling.1), custom_call_target="tpu_custom_call" | custom-call | tf_op jit(solution)/shard_map/pallas_call | solution.py:307
  10.1 0.0 collective-permute-done.before
  10.2 1.9 %collective-permute-start.1 = (f32[128,512]{1,0:T(8,128)S(1)}, f32[128,512]{1,0:T(8,128)S(1)}, u32[]{:S(2)}, u32[]{:S(2)}) collective-permute-start(f32[128,512]{1,0:T(8,128)S(1)} %get-tuple-element.33), channel_id=1, source_target_pairs={{1,2},{3,4},{5,6},{7,8},{9,10},{11,12},{13,14},{2,1},{4,3},{6,5},{... | collective-permute-start | bytes 786440 | tf_op jit(solution)/shard_map/ppermute | solution.py:304
  12.1 5.6 %collective-permute-start.2 = (f32[128,512]{1,0:T(8,128)S(1)}, f32[128,512]{1,0:T(8,128)S(1)}, u32[]{:S(2)}, u32[]{:S(2)}) collective-permute-start(f32[128,512]{1,0:T(8,128)S(1)} %get-tuple-element.34), channel_id=1, source_target_pairs={{0,1},{2,3},{4,5},{6,7},{8,9},{10,11},{12,13},{14,15},{1,0},{3,2},... | collective-permute-start | bytes 786440 | tf_op jit(solution)/shard_map/ppermute | solution.py:304
  17.7 0.2 collective-permute-done.1.odd_in
  17.8 1.0 collective-permute-done.2.even_in
  18.8 0.0 copy-start
  18.8 5.0 %shard_map.38 = (f32[128,256]{1,0:T(8,128)S(1)}, f32[128,256]{1,0:T(8,128)S(1)}, f32[128,256]{1,0:T(8,128)S(1)}, f32[128,512]{1,0:T(8,128)S(1)}) custom-call(f32[128,256]{1,0:T(8,128)S(1)} %get-tuple-element.28.diag, f32[128,256]{1,0:T(8,128)S(1)} %get-tuple-element.29.coupler, f32[1,2,128,128]{3,2,1,0:T(8,128)S(1)} %collective-permute-done.before, ...), custom_call_target="tpu_custom_call" | custom-call | tf_op jit(solution)/shard_map/pallas_call | solution.py:316
  23.8 1.9 %collective-permute-start.4 = (f32[128,512]{1,0:T(8,128)S(1)}, f32[128,512]{1,0:T(8,128)S(1)}, u32[]{:S(2)}, u32[]{:S(2)}) collective-permute-start(f32[128,512]{1,0:T(8,128)S(1)} %get-tuple-element.38), channel_id=1, source_target_pairs={{2,0},{3,1},{4,2},{5,3},{6,4},{7,5},{8,6},{9,7},{10,8},{11,9},{12,... | collective-permute-start | bytes 786440 | tf_op jit(solution)/shard_map/ppermute | solution.py:300
  25.8 4.7 %collective-permute-start.3 = (f32[128,512]{1,0:T(8,128)S(1)}, f32[128,512]{1,0:T(8,128)S(1)}, u32[]{:S(2)}, u32[]{:S(2)}) collective-permute-start(f32[128,512]{1,0:T(8,128)S(1)} %get-tuple-element.38), channel_id=1, source_target_pairs={{0,2},{1,3},{2,4},{3,5},{4,6},{5,7},{6,8},{7,9},{8,10},{9,11},{10,... | collective-permute-start | bytes 786440 | tf_op jit(solution)/shard_map/ppermute | solution.py:300
  30.5 4.9 %collective-permute-done.4.right = f32[128,512]{1,0:T(8,128)S(1)} collective-permute-done((f32[128,512]{1,0:T(8,128)S(1)}, f32[128,512]{1,0:T(8,128)S(1)}, u32[]{:S(2)}, u32[]{:S(2)}) %collective-permute-start.4) | collective-permute-done | bytes 262176 | tf_op jit(solution)/shard_map/ppermute | solution.py:300
  35.4 1.4 %collective-permute-done.3.left = f32[128,512]{1,0:T(8,128)S(1)} collective-permute-done((f32[128,512]{1,0:T(8,128)S(1)}, f32[128,512]{1,0:T(8,128)S(1)}, u32[]{:S(2)}, u32[]{:S(2)}) %collective-permute-start.3) | collective-permute-done | bytes 262176 | tf_op jit(solution)/shard_map/ppermute | solution.py:300
  36.8 5.0 %shard_map.39 = (f32[128,256]{1,0:T(8,128)S(1)}, f32[128,256]{1,0:T(8,128)S(1)}, f32[128,256]{1,0:T(8,128)S(1)}, f32[128,256]{1,0:T(8,128)S(1)}, f32[128,256]{1,0:T(8,128)S(1)}) custom-call(f32[128,256]{1,0:T(8,128)S(1)} %get-tuple-element.35.diag, f32[128,256]{1,0:T(8,128)S(1)} %get-tuple-element.36.lower, f32[128,256]{1,0:T(8,128)S(1)} %get-tuple-element.37.upper, ...), custom_call_target="tpu_custom_call" | custom-call | tf_op jit(solution)/shard_map/pallas_call | solution.py:324
  41.8 8.0 %collective-permute-start.5 = (f32[128,256]{1,0:T(8,128)S(1)}, f32[128,256]{1,0:T(8,128)S(1)}, u32[]{:S(2)}, u32[]{:S(2)}) collective-permute-start(f32[128,256]{1,0:T(8,128)S(1)} %get-tuple-element.42), channel_id=1, source_target_pairs={{0,4},{1,5},{2,6},{3,7},{4,8},{5,9},{6,10},{7,11},{8,12},{9,13},{1... | collective-permute-start | bytes 393224 | tf_op jit(solution)/shard_map/ppermute | solution.py:300
  49.7 1.9 %collective-permute-start.6 = (f32[128,256]{1,0:T(8,128)S(1)}, f32[128,256]{1,0:T(8,128)S(1)}, u32[]{:S(2)}, u32[]{:S(2)}) collective-permute-start(f32[128,256]{1,0:T(8,128)S(1)} %get-tuple-element.43), channel_id=1, source_target_pairs={{4,0},{5,1},{6,2},{7,3},{8,4},{9,5},{10,6},{11,7},{12,8},{13,9},{1... | collective-permute-start | bytes 393224 | tf_op jit(solution)/shard_map/ppermute | solution.py:300
  51.7 1.9 %collective-permute-start.8 = (f32[128,256]{1,0:T(8,128)S(1)}, f32[128,256]{1,0:T(8,128)S(1)}, u32[]{:S(2)}, u32[]{:S(2)}) collective-permute-start(f32[128,256]{1,0:T(8,128)S(1)} %get-tuple-element.42), channel_id=1, source_target_pairs={{4,0},{5,1},{6,2},{7,3},{8,4},{9,5},{10,6},{11,7},{20,16},{21,17},... | collective-permute-start | bytes 393224 | tf_op jit(solution)/shard_map/ppermute | solution.py:334
  53.6 6.0 %collective-permute-start.7 = (f32[128,256]{1,0:T(8,128)S(1)}, f32[128,256]{1,0:T(8,128)S(1)}, u32[]{:S(2)}, u32[]{:S(2)}) collective-permute-start(f32[128,256]{1,0:T(8,128)S(1)} %get-tuple-element.43), channel_id=1, source_target_pairs={{4,8},{5,9},{6,10},{7,11},{8,12},{9,13},{10,14},{11,15},{20,24},{2... | collective-permute-start | bytes 393224 | tf_op jit(solution)/shard_map/ppermute | solution.py:333
  59.6 0.0 collective-permute-done.5.left
  59.6 3.4 %collective-permute-done.6.right = f32[128,256]{1,0:T(8,128)S(1)} collective-permute-done((f32[128,256]{1,0:T(8,128)S(1)}, f32[128,256]{1,0:T(8,128)S(1)}, u32[]{:S(2)}, u32[]{:S(2)}) %collective-permute-start.6) | collective-permute-done | bytes 131104 | tf_op jit(solution)/shard_map/ppermute | solution.py:300
  63.1 4.9 %shard_map.40 = (f32[128,256]{1,0:T(8,128)S(1)}, f32[128,256]{1,0:T(8,128)S(1)}, f32[128,256]{1,0:T(8,128)S(1)}) custom-call(f32[128,256]{1,0:T(8,128)S(1)} %get-tuple-element.39.diag, f32[128,256]{1,0:T(8,128)S(1)} %get-tuple-element.40.lower, f32[128,256]{1,0:T(8,128)S(1)} %get-tuple-element.41.upper, f32[128,256]{1,0:T(8,128)S(1)} %collective-permute-done.5.left, ...), custom_call_target="tpu_custom_call" | custom-call | tf_op jit(solution)/shard_map/pallas_call | solution.py:335
  68.0 0.0 collective-permute-done.8.right_late
  68.0 0.0 copy-start.1
  68.0 0.0 collective-permute-done.7.left_late
  68.0 2.1 %collective-permute-start.9 = (f32[128,256]{1,0:T(8,128)S(1)}, f32[128,256]{1,0:T(8,128)S(1)}, u32[]{:S(2)}, u32[]{:S(2)}) collective-permute-start(f32[128,256]{1,0:T(8,128)S(1)} %get-tuple-element.49), channel_id=1, source_target_pairs={{0,8},{1,9},{2,10},{3,11},{4,12},{5,13},{6,14},{7,15},{8,0},{9,1},... | collective-permute-start | bytes 393224 | tf_op jit(solution)/shard_map/ppermute | solution.py:344
  70.2 1.5 %shard_map.41.hot = bf16[128,8192]{1,0:T(8,128)(2,1)S(1)} custom-call(s32[1,8192]{1,0:T(1,128)} %retained.2), custom_call_target="tpu_custom_call" | custom-call | tf_op jit(solution)/shard_map/pallas_call | solution.py:345
  71.7 9.1 %collective-permute-done.9.partner = f32[128,256]{1,0:T(8,128)S(1)} collective-permute-done((f32[128,256]{1,0:T(8,128)S(1)}, f32[128,256]{1,0:T(8,128)S(1)}, u32[]{:S(2)}, u32[]{:S(2)}) %collective-permute-start.9) | collective-permute-done | bytes 131104 | tf_op jit(solution)/shard_map/ppermute | solution.py:344
  80.7 0.0 copy-done.1
  80.8 0.0 copy-done
  80.8 0.0 copy-start.2
  80.8 0.9 copy-done.2
  81.7 7.7 %shard_map.42 = f32[32,8,128]{2,1,0:T(8,128)S(1)} custom-call(f32[128,256]{1,0:T(8,128)S(1)} %get-tuple-element.44.diag, f32[128,256]{1,0:T(8,128)S(1)} %get-tuple-element.45.side, f32[128,256]{1,0:T(8,128)S(1)} %collective-permute-done.5.left, f32[128,256]{1,0:T(8,128)S(1)} %collective-permute-done.6.right, ...), custom_call_target="tpu_custom_call" | custom-call | tf_op jit(solution)/shard_map/pallas_call | solution.py:351
  89.4 20.3 %all_to_all.5 = f32[32,8,128]{2,1,0:T(8,128)S(1)} all-to-all(f32[32,8,128]{2,1,0:T(8,128)S(1)} %shard_map.42), channel_id=1, replica_groups=mesh['energy'=32,'chain'=16] {'energy'}, dimensions={0} | all-to-all | bytes 262144 | tf_op jit(solution)/shard_map/all_to_all | solution.py:370
  109.7 1.0 shard_map.43
Async XLA Ops:
  0.0 10.1 %collective-permute-start = (f32[1,2,128,128]{3,2,1,0:T(8,128)}, f32[1,2,128,128]{3,2,1,0:T(8,128)S(1)}, u32[]{:S(2)}, u32[]{:S(2)}) collective-permute-start(f32[1,2,128,128]{3,2,1,0:T(8,128)} %coupling.1), channel_id=1, source_target_pairs={{0,2},{1,3},{2,4},{3,5},{4,6},{5,7},{6,8},{7,9},{8,10},{9,11},{10,... | collective-permute-start | bytes 393224 | tf_op jit(solution)/shard_map/ppermute | solution.py:300
  10.2 7.7 %collective-permute-start.1 = (f32[128,512]{1,0:T(8,128)S(1)}, f32[128,512]{1,0:T(8,128)S(1)}, u32[]{:S(2)}, u32[]{:S(2)}) collective-permute-start(f32[128,512]{1,0:T(8,128)S(1)} %get-tuple-element.33), channel_id=1, source_target_pairs={{1,2},{3,4},{5,6},{7,8},{9,10},{11,12},{13,14},{2,1},{4,3},{6,5},{... | collective-permute-start | bytes 786440 | tf_op jit(solution)/shard_map/ppermute | solution.py:304
  12.1 6.7 %collective-permute-start.2 = (f32[128,512]{1,0:T(8,128)S(1)}, f32[128,512]{1,0:T(8,128)S(1)}, u32[]{:S(2)}, u32[]{:S(2)}) collective-permute-start(f32[128,512]{1,0:T(8,128)S(1)} %get-tuple-element.34), channel_id=1, source_target_pairs={{0,1},{2,3},{4,5},{6,7},{8,9},{10,11},{12,13},{14,15},{1,0},{3,2},... | collective-permute-start | bytes 786440 | tf_op jit(solution)/shard_map/ppermute | solution.py:304
  18.8 61.9 %copy-start = (s32[1,8192]{1,0:T(1,128)S(1)}, s32[1,8192]{1,0:T(1,128)}, u32[]{:S(2)}) copy-start(s32[1,8192]{1,0:T(1,128)} %retained.2) | copy-start | bytes 98308
  23.8 11.6 %collective-permute-start.4 = (f32[128,512]{1,0:T(8,128)S(1)}, f32[128,512]{1,0:T(8,128)S(1)}, u32[]{:S(2)}, u32[]{:S(2)}) collective-permute-start(f32[128,512]{1,0:T(8,128)S(1)} %get-tuple-element.38), channel_id=1, source_target_pairs={{2,0},{3,1},{4,2},{5,3},{6,4},{7,5},{8,6},{9,7},{10,8},{11,9},{12,... | collective-permute-start | bytes 786440 | tf_op jit(solution)/shard_map/ppermute | solution.py:300
  25.8 11.0 %collective-permute-start.3 = (f32[128,512]{1,0:T(8,128)S(1)}, f32[128,512]{1,0:T(8,128)S(1)}, u32[]{:S(2)}, u32[]{:S(2)}) collective-permute-start(f32[128,512]{1,0:T(8,128)S(1)} %get-tuple-element.38), channel_id=1, source_target_pairs={{0,2},{1,3},{2,4},{3,5},{4,6},{5,7},{6,8},{7,9},{8,10},{9,11},{10,... | collective-permute-start | bytes 786440 | tf_op jit(solution)/shard_map/ppermute | solution.py:300
  41.8 17.9 %collective-permute-start.5 = (f32[128,256]{1,0:T(8,128)S(1)}, f32[128,256]{1,0:T(8,128)S(1)}, u32[]{:S(2)}, u32[]{:S(2)}) collective-permute-start(f32[128,256]{1,0:T(8,128)S(1)} %get-tuple-element.42), channel_id=1, source_target_pairs={{0,4},{1,5},{2,6},{3,7},{4,8},{5,9},{6,10},{7,11},{8,12},{9,13},{1... | collective-permute-start | bytes 393224 | tf_op jit(solution)/shard_map/ppermute | solution.py:300
  49.7 13.4 %collective-permute-start.6 = (f32[128,256]{1,0:T(8,128)S(1)}, f32[128,256]{1,0:T(8,128)S(1)}, u32[]{:S(2)}, u32[]{:S(2)}) collective-permute-start(f32[128,256]{1,0:T(8,128)S(1)} %get-tuple-element.43), channel_id=1, source_target_pairs={{4,0},{5,1},{6,2},{7,3},{8,4},{9,5},{10,6},{11,7},{12,8},{13,9},{1... | collective-permute-start | bytes 393224 | tf_op jit(solution)/shard_map/ppermute | solution.py:300
  51.7 16.3 %collective-permute-start.8 = (f32[128,256]{1,0:T(8,128)S(1)}, f32[128,256]{1,0:T(8,128)S(1)}, u32[]{:S(2)}, u32[]{:S(2)}) collective-permute-start(f32[128,256]{1,0:T(8,128)S(1)} %get-tuple-element.42), channel_id=1, source_target_pairs={{4,0},{5,1},{6,2},{7,3},{8,4},{9,5},{10,6},{11,7},{20,16},{21,17},... | collective-permute-start | bytes 393224 | tf_op jit(solution)/shard_map/ppermute | solution.py:334
  53.6 14.4 %collective-permute-start.7 = (f32[128,256]{1,0:T(8,128)S(1)}, f32[128,256]{1,0:T(8,128)S(1)}, u32[]{:S(2)}, u32[]{:S(2)}) collective-permute-start(f32[128,256]{1,0:T(8,128)S(1)} %get-tuple-element.43), channel_id=1, source_target_pairs={{4,8},{5,9},{6,10},{7,11},{8,12},{9,13},{10,14},{11,15},{20,24},{2... | collective-permute-start | bytes 393224 | tf_op jit(solution)/shard_map/ppermute | solution.py:333
  68.0 12.8 %copy-start.1 = (f32[128,256]{1,0:T(8,128)}, f32[128,256]{1,0:T(8,128)S(1)}, u32[]{:S(2)}) copy-start(f32[128,256]{1,0:T(8,128)S(1)} %collective-permute-done.8.right_late) | copy-start | bytes 393220
  68.0 12.7 %collective-permute-start.9 = (f32[128,256]{1,0:T(8,128)S(1)}, f32[128,256]{1,0:T(8,128)S(1)}, u32[]{:S(2)}, u32[]{:S(2)}) collective-permute-start(f32[128,256]{1,0:T(8,128)S(1)} %get-tuple-element.49), channel_id=1, source_target_pairs={{0,8},{1,9},{2,10},{3,11},{4,12},{5,13},{6,14},{7,15},{8,0},{9,1},... | collective-permute-start | bytes 393224 | tf_op jit(solution)/shard_map/ppermute | solution.py:344
  80.8 0.9 copy-start.2
